TPU v7x, 32 devices: a whole 2x2x4 slice. The times are simulated.
32 devices in a mesh: leaf: 8 (over z, core), sub: 4 (over y, x).
Axes of the slice: x: 2, y: 2, z: 4, core: 2. Of those that a mesh axis runs over, the one named last changes fastest.
Arguments:
- leaf_maps: float32 [32, 256, 1024], P('leaf', 'sub'), may hold values from -8 to 28, as said below
- order_one: int32 [8, 4], replicated, may hold values from 0 to 3, each once within a row
- order_two: int32 [4, 6], replicated, may hold values from 0 to 5, each once within a row
- top_data: float32 [16, 256, 256], P('leaf', 'sub'), may hold values from -6 to 6
Outputs:
- top_map: float32 [16, 256, 2048], P('leaf', 'sub')
- leaf_data: float32 [32, 256, 256], P('leaf', 'sub')
Inputs may be any that keep to these rules, and one draw needn't show every extreme that they name: Each leaf's block of 1024 rows of leaf_maps, read as a 1024 by 1024 matrix, is symmetric and positive definite.
All inputs are finite; a program needn't handle non-finite values. Where the computation divides by a largest or mean magnitude, that divisor is 1e-20 or more.
Results may differ from a plain program's by a relative error of at most 0.0001.
Values sent between devices are 32-bit elements; how exact they have to be, the bound alone decides.
No kernel may reach another device: no remote copies, remote signals or barrier semaphores. Data moves between devices by JAX's collectives and lax.ppermute only.
A program may use at most 64 MiB of HBM per device.

v0:
```python
import jax
import jax.numpy as jnp
from jax import lax
from jax.experimental import pallas as pl
from jax.experimental.pallas import tpu as pltpu
from jax.sharding import PartitionSpec as P


W = 256
K = 256
F32 = jnp.float32
BF16 = jnp.bfloat16
NN = (((1,), (0,)), ((), ()))
NT = (((1,), (1,)), ((), ()))

VMEM_MIB = 24


def swapped(value, axis, mask):
    pairs = [(source, source ^ mask) for source in range(lax.axis_size(axis))]
    return lax.ppermute(value, axis, pairs)


def parts_of(value):
    high = value.astype(BF16)
    return high, (value - high.astype(F32)).astype(BF16)


def product(left, right, dims=NN):
    left_high, left_low = left if isinstance(left, tuple) else parts_of(left)
    right_high, right_low = right if isinstance(right, tuple) else parts_of(right)

    def one(a, b):
        return lax.dot_general(a, b, dims, preferred_element_type=F32)

    return one(left_high, right_low) + one(left_low, right_high) + one(left_high, right_high)


def newton(block):
    size = block.shape[0]
    bound = jnp.max(jnp.sum(jnp.abs(block), axis=1, keepdims=True), axis=0, keepdims=True)
    inverse_bound = 1.0 / bound
    rows = lax.broadcasted_iota(jnp.int32, (size, size), 0)
    columns = lax.broadcasted_iota(jnp.int32, (size, size), 1)
    eye = (rows == columns).astype(F32)
    power = eye - block * inverse_bound
    total = (eye + power) * inverse_bound
    split = parts_of(power)
    for _ in range(3):
        power = product(split, split)
        split = parts_of(power)
        total = total + product(total, split)
    return total


class Tree:
    def __init__(self, order_one, order_two):
        self.leaf = lax.axis_index("leaf")
        self.member = lax.axis_index("sub")
        self.half = self.leaf % 2
        self.node = self.leaf // 2
        self.order_one = order_one
        self.order_two = order_two

    def edge(self, position):
        joint = self.order_two[self.node, position]
        which = joint // 3
        return which, self.order_one[2 * self.node + which, joint % 3]

    def inner(self, which):
        return self.order_one[2 * self.node + which, 3]


def block_of(tree, own, other, which, row_edge, start, size, column_edge):
    column = pl.ds(pl.multiple_of(column_edge * W, W), W)
    rows = pl.ds(start, size)
    return jnp.where(which == tree.half, own[row_edge, rows, column], other[row_edge, rows, column])


def first_kernel(order_one, order_two, own, other, piece, coupling, coupling_own):
    tree = Tree(order_one, order_two)
    half_width = piece.shape[1]
    width = coupling.shape[1]
    start = pl.multiple_of(tree.half * half_width, half_width)
    total = None
    for which in range(2):
        inner = tree.inner(which)
        part = block_of(tree, own, other, which, inner, start, half_width, inner)
        total = part if total is None else total + part
    piece[0] = total
    for slot in range(2):
        which, edge = tree.edge(4 + slot)
        piece[1 + slot] = block_of(tree, own, other, which, edge, start, half_width, tree.inner(which))
    for slot in range(4):
        which, edge = tree.edge(slot)
        coupling[slot] = block_of(tree, own, other, which, edge, 0, width, tree.inner(which))
    for slot in range(2):
        coupling_own[slot] = coupling[2 * tree.half + slot]


def interface_rows(tree, own, other, position, start, size):
    which, edge = tree.edge(position)
    found = []
    for slot in range(2):
        column_which, column_edge = tree.edge(4 + slot)
        value = block_of(tree, own, other, which, edge, start, size, column_edge)
        found.append(jnp.where(which == column_which, value, 0.0))
    return jnp.concatenate(found, axis=1)


def second_kernel(count, order_one, order_two, own, other, *refs):
    pieces, (inner_rows, inverse_out, coupling_inner, right_out, sums) = refs[: 2 * count], refs[2 * count :]
    tree = Tree(order_one, order_two)
    half_width = pieces[0].shape[1]
    width = 2 * half_width
    for mask in range(count):
        for side in range(2):
            piece = pieces[2 * mask + side]
            row = (tree.member ^ mask) * width + (tree.half ^ side) * half_width
            sums[pl.ds(pl.multiple_of(row, half_width), half_width), :] = piece[0]
            for slot in range(2):
                target = pl.ds(pl.multiple_of(row + slot * W, half_width), half_width)
                coupling_inner[target, :] = piece[1 + slot]
    inverse = newton(sums[...])
    inverse_out[...] = inverse
    right = product(inverse, coupling_inner[...], NT)
    right_out[...] = right
    start = pl.multiple_of(tree.half * half_width, half_width)
    left = jnp.concatenate([pieces[0][1], pieces[0][2]], axis=0)
    change = product(left, right)
    for slot in range(2):
        rows = slice(slot * half_width, (slot + 1) * half_width)
        inner_rows[rows, :] = interface_rows(tree, own, other, 4 + slot, start, half_width) - change[rows]


def outer_kernel(order_one, order_two, own, other, coupling, right, outer_all, outer_own):
    tree = Tree(order_one, order_two)
    width = coupling.shape[1]
    change = product(coupling[...].reshape(4 * width, W), right[...])
    for slot in range(4):
        base = interface_rows(tree, own, other, slot, 0, width)
        outer_all[slot] = base - change[slot * width : (slot + 1) * width]
    for slot in range(2):
        outer_own[slot] = outer_all[2 * tree.half + slot]


def third_kernel(count, *refs):
    pieces, (inverse_out, sums) = refs[: 2 * count], refs[2 * count :]
    half, member = lax.axis_index("leaf") % 2, lax.axis_index("sub")
    half_width = pieces[0].shape[0] // 2
    width = 2 * half_width
    for mask in range(count):
        for side in range(2):
            piece = pieces[2 * mask + side]
            row = (member ^ mask) * width + (half ^ side) * half_width
            for slot in range(2):
                target = pl.ds(pl.multiple_of(row + slot * W, half_width), half_width)
                sums[target, :] = piece[slot * half_width : (slot + 1) * half_width, :]
    inverse_out[...] = newton(sums[...])


def near_kernel(count, order_one, order_two, own, other, coupling, inverse_one, *refs):
    bulks, (base_out, driven_one, coupling_half, data_half) = refs[:count], refs[count:]
    tree = Tree(order_one, order_two)
    node_bit = tree.node % 2
    width = own.shape[1]
    for mask in range(count):
        at = (tree.member ^ mask) * width
        for slot in range(2):
            row = pl.multiple_of(slot * W + at, width)
            coupling_half[pl.ds(row, width), :] = bulks[mask][4 + slot]
            for far in range(2):
                row = pl.multiple_of((2 * (node_bit ^ far) + slot) * W + at, width)
                data_half[pl.ds(row, width), :] = bulks[mask][2 * far + slot]
    coupling_split = parts_of(coupling_half[...])
    scaled = product(coupling[...].reshape(4 * width, W), inverse_one[...])
    local = product(scaled, coupling_split, NT)
    for slot in range(4):
        which, edge = tree.edge(slot)
        for column in range(2):
            column_which, column_edge = tree.edge(2 * tree.half + column)
            value = block_of(tree, own, other, which, edge, 0, width, column_edge)
            value = jnp.where(which == column_which, value, 0.0)
            rows, columns = slice(slot * width, (slot + 1) * width), slice(column * W, (column + 1) * W)
            base_out[slot, :, columns] = value - local[rows, columns]
    near = data_half[pl.ds(pl.multiple_of(node_bit * 2 * W, W), 2 * W), :]
    driven_one[...] = product(near.T, coupling_split)


def far_kernel(count, data_half, driven_one, *refs):
    outers, (driven, outer_half) = refs[: 2 * count], refs[2 * count :]
    node_bit, member = (lax.axis_index("leaf") // 2) % 2, lax.axis_index("sub")
    width = outers[0].shape[1]
    for mask in range(count):
        at = (member ^ mask) * width
        for slot in range(2):
            for far in range(2):
                row = pl.multiple_of((2 * (node_bit ^ far) + slot) * W + at, width)
                outer_half[pl.ds(row, width), :] = outers[mask + far * count][slot]
    driven[:, : 2 * W] = product(data_half[...].T, outer_half[...])
    driven[:, 2 * W :] = driven_one[...]


def top_kernel(base, outer_all, inverse_two, outer_half, mine, theirs):
    half, node_bit = lax.axis_index("leaf") % 2, (lax.axis_index("leaf") // 2) % 2
    slots, width, columns = base.shape
    scaled = product(outer_all[...].reshape(slots * width, columns), inverse_two[...])
    change = -product(scaled, outer_half[...], NT)
    for bit in range(2):
        held = jnp.where(bit == node_bit, base[...], 0.0)
        part = held + change[:, bit * columns : (bit + 1) * columns].reshape(slots, width, columns)
        mine[:, :, bit * columns : (bit + 1) * columns] = jnp.where(half == 0, part[:2], part[2:])
        theirs[:, :, bit * columns : (bit + 1) * columns] = jnp.where(half == 0, part[2:], part[:2])


def leaf_kernel(order_one, order_two, data_own, data_other, coupling_inner, inverse_one, inverse_two, driven, driven_other, leaf_data, inner):
    tree = Tree(order_one, order_two)
    width = leaf_data.shape[1]
    total = driven[...] + driven_other[...]
    second = parts_of(total[:, : 2 * W])
    lifted = -product(second, inverse_two[...])
    first = total[:, 2 * W :] + product(lifted, coupling_inner[...])
    mine = pl.multiple_of(tree.member * width, width)
    rows = [inverse_two[pl.ds(pl.multiple_of(slot * W + mine, width), width), :] for slot in range(2)]
    inner[...] = -product(jnp.concatenate(rows, axis=0), second, NT)
    leaf_data[tree.order_one[tree.leaf, 3]] = -product(inverse_one[pl.ds(mine, width), :], first, NT)
    for slot in range(3):
        joint = 3 * tree.half + slot
        position = 0
        for place in range(6):
            position = position + place * (order_two[tree.node, place] == joint).astype(jnp.int32)
        place = position % 2
        from_data = jnp.where(position // 2 == tree.half, data_own[place], data_other[place])
        from_inner = inner[pl.ds(pl.multiple_of(place * width, width), width), :]
        leaf_data[order_one[tree.leaf, slot]] = jnp.where(position < 4, from_data, from_inner)


def join_kernel(mine, theirs, top_map):
    half = lax.axis_index("leaf") % 2
    columns = mine.shape[2] // 2
    for bit in range(2):
        source = slice(bit * columns, (bit + 1) * columns)
        for side, held in enumerate((mine, theirs)):
            target = pl.multiple_of((2 * bit + (half ^ side)) * columns, columns)
            top_map[:, :, pl.ds(target, columns)] = held[:, :, source]


def call(kernel, scalar_count, outs, scratch, *args):
    smem = pl.BlockSpec(memory_space=pltpu.SMEM)
    vmem = pl.BlockSpec(memory_space=pltpu.VMEM)
    return pl.pallas_call(
        kernel,
        in_specs=[smem] * scalar_count + [vmem] * (len(args) - scalar_count),
        out_specs=[vmem] * len(outs),
        out_shape=[jax.ShapeDtypeStruct(shape, F32) for shape in outs],
        scratch_shapes=[pltpu.VMEM(shape, F32) for shape in scratch],
        compiler_params=pltpu.CompilerParams(vmem_limit_bytes=VMEM_MIB * 2**20),
    )(*args)


def shards(leaf_maps, order_one, order_two, top_data):
    width = leaf_maps.shape[1]
    half_width = width // 2
    count = lax.axis_size("sub")
    bits = [("sub", 2**bit) for bit in range((count - 1).bit_length())] + [("leaf", 2)]
    orders = (order_one, order_two)

    def across(value):
        found = {0: value}
        for mask in sorted(range(1, count), key=lambda m: (-bin(m).count("1"), m)):
            found[mask] = swapped(value, "sub", mask)
        return [found[mask] for mask in range(count)]

    def spread(value, used):
        found = {0: value}
        for mask in sorted(range(1, 2 ** len(used)), key=lambda m: (bin(m).count("1"), m)):
            held = [bit for bit in range(len(used)) if mask >> bit & 1]
            chosen = next((bit for bit in held if (bit + 1) % len(used) in held), held[0])
            found[mask] = swapped(found[mask ^ (1 << chosen)], *used[chosen])
        return [found[mask] for mask in range(2 ** len(used))]

    def with_sibling(values):
        return [item for value in values for item in (value, swapped(value, "leaf", 1))]

    other = swapped(leaf_maps, "leaf", 1)
    data_far = swapped(top_data, "leaf", 2)
    piece, coupling, coupling_own = call(
        first_kernel, 2, [(3, half_width, W), (4, width, W), (2, width, W)], [], *orders, leaf_maps, other
    )
    pieces = with_sibling(across(piece))
    data_other = swapped(top_data, "leaf", 1)
    bulks = spread(jnp.concatenate([top_data, data_far, coupling_own], axis=0), bits[:-1])
    inner_rows, inverse_one, coupling_inner, right = call(
        lambda *refs: second_kernel(count, *refs), 2,
        [(2 * half_width, 2 * W), (W, W), (2 * W, W), (W, 2 * W)], [(W, W)],
        *orders, leaf_maps, other, *pieces,
    )
    summed = inner_rows + swapped(inner_rows, "leaf", 2)
    outer_all, outer_own = call(
        outer_kernel, 2, [(4, width, 2 * W), (2, width, 2 * W)], [], *orders, leaf_maps, other, coupling, right
    )
    outers = spread(outer_own, bits)
    (inverse_two,) = call(
        lambda *refs: third_kernel(count, *refs), 0, [(2 * W, 2 * W)], [(2 * W, 2 * W)],
        *with_sibling(across(summed)),
    )
    base, driven_one, _, data_half = call(
        lambda *refs: near_kernel(count, *refs), 2,
        [(4, width, 2 * W), (K, W), (2 * W, W), (4 * W, K)], [], *orders, leaf_maps, other, coupling, inverse_one, *bulks,
    )
    driven, outer_half = call(
        lambda *refs: far_kernel(count, *refs), 0, [(K, 3 * W), (4 * W, 2 * W)], [], data_half, driven_one, *outers
    )
    driven_other = swapped(driven, "leaf", 1)
    mine, theirs = call(top_kernel, 0, [(2, width, 4 * W)] * 2, [], base, outer_all, inverse_two, outer_half)
    received = swapped(theirs, "leaf", 1)
    (leaf_data,) = call(
        leaf_kernel, 2, [(4, width, K)], [(2 * width, K)],
        *orders, top_data, data_other, coupling_inner, inverse_one, inverse_two, driven, driven_other,
    )
    (top_map,) = call(join_kernel, 0, [(2, width, 8 * W)], [], mine, received)
    return (top_map, leaf_data)


def solution(mesh):
    in_specs = (P("leaf", "sub", None), P(), P(), P("leaf", "sub", None))
    out_specs = (P("leaf", "sub", None), P("leaf", "sub", None))

    return jax.shard_map(shards, mesh=mesh, in_specs=in_specs, out_specs=out_specs, check_vma=False)
```

profile of v0, /device:TPU:0, one launch (start us, length us, event | category | flops | bytes accessed | tf_op | source)
XLA Modules:
  0.0 84.2 jit_solution(7184102487720736695)
XLA Ops:
  1.2 2.6 %collective-permute-start.8 = (f32[2,64,256]{2,1,0:T(8,128)}, f32[2,64,256]{2,1,0:T(8,128)S(1)}, u32[]{:S(2)}, u32[]{:S(2)}) collective-permute-start(f32[2,64,256]{2,1,0:T(8,128)} %data_own.1), channel_id=1, source_target_pairs={{0,8},{4,12},{8,0},{12,4},{16,24},{20,28},{24,16},{28,20},{1,9},{5... | collective-permute-start | bytes 393224 | tf_op jit(solution)/shard_map/ppermute | solution.py:21
  5.5 1.2 %copy-done = f32[4,64,1024]{2,1,0:T(8,128)S(1)} copy-done((f32[4,64,1024]{2,1,0:T(8,128)S(1)}, f32[4,64,1024]{2,1,0:T(8,128)}, u32[]{:S(2)}) %copy-start) | copy-done | bytes 1048600
  8.2 1.6 %collective-permute-start.2 = (f32[3,32,256]{2,1,0:T(8,128)S(1)}, f32[3,32,256]{2,1,0:T(8,128)S(1)}, u32[]{:S(2)}, u32[]{:S(2)}) collective-permute-start(f32[3,32,256]{2,1,0:T(8,128)S(1)} %get-tuple-element.19.refs_4_), channel_id=1, source_target_pairs={{0,1},{1,0},{2,3},{3,2},{4,5},{5,4},{6,7},{7,6},{8,9},{9,8},{10,11... | collective-permute-start | bytes 294920 | tf_op jit(solution)/shard_map/ppermute | solution.py:21
  9.7 1.5 %collective-permute-start.4 = (f32[3,32,256]{2,1,0:T(8,128)S(1)}, f32[3,32,256]{2,1,0:T(8,128)S(1)}, u32[]{:S(2)}, u32[]{:S(2)}) collective-permute-start(f32[3,32,256]{2,1,0:T(8,128)S(1)} %get-tuple-element.19.refs_4_), channel_id=1, source_target_pairs={{0,2},{1,3},{2,0},{3,1},{4,6},{5,7},{6,4},{7,5},{8,10},{9,11},{10,... | collective-permute-start | bytes 294920 | tf_op jit(solution)/shard_map/ppermute | solution.py:21
  11.8 1.3 %collective-permute-done.2.refs_6_ = f32[3,32,256]{2,1,0:T(8,128)S(1)} collective-permute-done((f32[3,32,256]{2,1,0:T(8,128)S(1)}, f32[3,32,256]{2,1,0:T(8,128)S(1)}, u32[]{:S(2)}, u32[]{:S(2)}) %collective-permute-start.2) | collective-permute-done | bytes 98336 | tf_op jit(solution)/shard_map/ppermute | solution.py:21
  13.1 2.4 %collective-permute-done.4.refs_8_ = f32[3,32,256]{2,1,0:T(8,128)S(1)} collective-permute-done((f32[3,32,256]{2,1,0:T(8,128)S(1)}, f32[3,32,256]{2,1,0:T(8,128)S(1)}, u32[]{:S(2)}, u32[]{:S(2)}) %collective-permute-start.4) | collective-permute-done | bytes 98336 | tf_op jit(solution)/shard_map/ppermute | solution.py:21
  15.5 1.3 %collective-permute-done.6.refs_10_ = f32[3,32,256]{2,1,0:T(8,128)S(1)} collective-permute-done((f32[3,32,256]{2,1,0:T(8,128)S(1)}, f32[3,32,256]{2,1,0:T(8,128)S(1)}, u32[]{:S(2)}, u32[]{:S(2)}) %collective-permute-start.6) | collective-permute-done | bytes 98336 | tf_op jit(solution)/shard_map/ppermute | solution.py:21
  16.8 1.8 %collective-permute-start.10 = (f32[6,64,256]{2,1,0:T(8,128)S(1)}, f32[6,64,256]{2,1,0:T(8,128)S(1)}, u32[]{:S(2)}, u32[]{:S(2)}) collective-permute-start(f32[6,64,256]{2,1,0:T(8,128)S(1)} %constant_dynamic-update-slice_fusion.refs_6_), channel_id=1, source_target_pairs={{0,2},{1,3},{2,0},{3,1},{4,6},{5,7},{6,4},{7,5},{8,10},{9,11},{10,... | collective-permute-start | bytes 1179656 | tf_op jit(solution)/shard_map/ppermute | solution.py:21
  18.6 2.7 %shard_map.60 = (f32[64,512]{1,0:T(8,128)S(1)}, f32[256,256]{1,0:T(8,128)S(1)}, f32[512,256]{1,0:T(8,128)S(1)}, f32[256,512]{1,0:T(8,128)S(1)}) custom-call(s32[8,4]{1,0:T(8,128)S(1)} %copy.8.order_one.refs_0_, s32[4,6]{1,0:T(4,128)S(1)} %copy-done.2, f32[4,64,1024]{2,1,0:T(8,128)S(1)} %copy-done, f32[4,64,1024]{2,1,0:T(8,128)S(1)} %collective-permute-done.other.refs_3_, ...), custom_call_target="tpu_custom_call" | custom-call | tf_op jit(solution)/shard_map/pallas_call | solution.py:251
  22.4 1.2 %collective-permute-start.23 = (f32[2,64,512]{2,1,0:T(8,128)S(1)}, f32[2,64,512]{2,1,0:T(8,128)S(1)}, u32[]{:S(2)}, u32[]{:S(2)}) collective-permute-start(f32[2,64,512]{2,1,0:T(8,128)S(1)} %get-tuple-element.28.refs_2_), channel_id=1, source_target_pairs={{0,8},{4,12},{8,0},{12,4},{16,24},{20,28},{24,16},{28,20},{1,9},{5... | collective-permute-start | bytes 786440 | tf_op jit(solution)/shard_map/ppermute | solution.py:21
  25.8 5.8 %collective-permute-done.23.refs_6_ = f32[2,64,512]{2,1,0:T(8,128)S(1)} collective-permute-done((f32[2,64,512]{2,1,0:T(8,128)S(1)}, f32[2,64,512]{2,1,0:T(8,128)S(1)}, u32[]{:S(2)}, u32[]{:S(2)}) %collective-permute-start.23) | collective-permute-done | bytes 262176 | tf_op jit(solution)/shard_map/ppermute | solution.py:21
  33.9 1.3 %collective-permute-start.11 = (f32[6,64,256]{2,1,0:T(8,128)S(1)}, f32[6,64,256]{2,1,0:T(8,128)S(1)}, u32[]{:S(2)}, u32[]{:S(2)}) collective-permute-start(f32[6,64,256]{2,1,0:T(8,128)S(1)} %collective-permute-done.10.refs_8_), channel_id=1, source_target_pairs={{0,1},{1,0},{2,3},{3,2},{4,5},{5,4},{6,7},{7,6},{8,9},{9,8},{10,11... | collective-permute-start | bytes 1179656 | tf_op jit(solution)/shard_map/ppermute | solution.py:21
  37.1 2.5 %collective-permute-done.25.refs_8_ = f32[2,64,512]{2,1,0:T(8,128)S(1)} collective-permute-done((f32[2,64,512]{2,1,0:T(8,128)S(1)}, f32[2,64,512]{2,1,0:T(8,128)S(1)}, u32[]{:S(2)}, u32[]{:S(2)}) %collective-permute-start.25) | collective-permute-done | bytes 262176 | tf_op jit(solution)/shard_map/ppermute | solution.py:21
  40.5 4.7 %collective-permute-done.9.refs_7_ = f32[6,64,256]{2,1,0:T(8,128)S(1)} collective-permute-done((f32[6,64,256]{2,1,0:T(8,128)S(1)}, f32[6,64,256]{2,1,0:T(8,128)S(1)}, u32[]{:S(2)}, u32[]{:S(2)}) %collective-permute-start.9) | collective-permute-done | bytes 393248 | tf_op jit(solution)/shard_map/ppermute | solution.py:21
  45.9 13.3 %collective-permute-done.22.refs_5_ = f32[2,64,512]{2,1,0:T(8,128)S(1)} collective-permute-done((f32[2,64,512]{2,1,0:T(8,128)S(1)}, f32[2,64,512]{2,1,0:T(8,128)S(1)}, u32[]{:S(2)}, u32[]{:S(2)}) %collective-permute-start.22) | collective-permute-done | bytes 262176 | tf_op jit(solution)/shard_map/ppermute | solution.py:21
  59.2 1.5 %collective-permute-start.16 = (f32[64,512]{1,0:T(8,128)S(1)}, f32[64,512]{1,0:T(8,128)S(1)}, u32[]{:S(2)}, u32[]{:S(2)}) collective-permute-start(f32[64,512]{1,0:T(8,128)S(1)} %add.3.refs_0_), channel_id=1, source_target_pairs={{0,2},{1,3},{2,0},{3,1},{4,6},{5,7},{6,4},{7,5},{8,10},{9,11},{10,... | collective-permute-start | bytes 393224 | tf_op jit(solution)/shard_map/ppermute | solution.py:21
  61.4 2.2 %shard_map.61 = (f32[4,64,512]{2,1,0:T(8,128)S(1)}, f32[256,256]{1,0:T(8,128)S(1)}, f32[512,256]{1,0:T(8,128)}, f32[1024,256]{1,0:T(8,128)S(1)}) custom-call(s32[8,4]{1,0:T(8,128)S(1)} %copy.8.order_one.refs_0_, s32[4,6]{1,0:T(4,128)S(1)} %copy-done.2, f32[4,64,1024]{2,1,0:T(8,128)S(1)} %copy-done, f32[4,64,1024]{2,1,0:T(8,128)S(1)} %collective-permute-done.other.refs_3_, ...), custom_call_target="tpu_custom_call" | custom-call | tf_op jit(solution)/shard_map/pallas_call | solution.py:251
  63.6 1.2 %collective-permute-done.26.refs_9_ = f32[2,64,512]{2,1,0:T(8,128)S(1)} collective-permute-done((f32[2,64,512]{2,1,0:T(8,128)S(1)}, f32[2,64,512]{2,1,0:T(8,128)S(1)}, u32[]{:S(2)}, u32[]{:S(2)}) %collective-permute-start.26) | collective-permute-done | bytes 262176 | tf_op jit(solution)/shard_map/ppermute | solution.py:21
  67.4 2.4 %collective-permute-done.18.refs_6_ = f32[64,512]{1,0:T(8,128)S(1)} collective-permute-done((f32[64,512]{1,0:T(8,128)S(1)}, f32[64,512]{1,0:T(8,128)S(1)}, u32[]{:S(2)}, u32[]{:S(2)}) %collective-permute-start.18) | collective-permute-done | bytes 131104 | tf_op jit(solution)/shard_map/ppermute | solution.py:21
  69.9 1.3 %collective-permute-done.19.refs_7_ = f32[64,512]{1,0:T(8,128)S(1)} collective-permute-done((f32[64,512]{1,0:T(8,128)S(1)}, f32[64,512]{1,0:T(8,128)S(1)}, u32[]{:S(2)}, u32[]{:S(2)}) %collective-permute-start.19) | collective-permute-done | bytes 131104 | tf_op jit(solution)/shard_map/ppermute | solution.py:21
  71.2 5.7 %shard_map.63.inverse_two = f32[512,512]{1,0:T(8,128)S(1)} custom-call(f32[64,512]{1,0:T(8,128)S(1)} %add.3.refs_0_, f32[64,512]{1,0:T(8,128)S(1)} %collective-permute-done.13.refs_1_, f32[64,512]{1,0:T(8,128)S(1)} %collective-permute-done.14.refs_2_, f32[64,512]{1,0:T(8,128)S(1)} %collective-permute-done.15.refs_3_, ...), custom_call_target="tpu_custom_call" | custom-call | tf_op jit(solution)/shard_map/pallas_call | solution.py:251
  76.9 1.5 %shard_map.65 = (f32[2,64,1024]{2,1,0:T(8,128)S(1)}, f32[2,64,1024]{2,1,0:T(8,128)S(1)}) custom-call(f32[4,64,512]{2,1,0:T(8,128)S(1)} %get-tuple-element.22.base, f32[4,64,512]{2,1,0:T(8,128)S(1)} %get-tuple-element.24.outer_all, f32[512,512]{1,0:T(8,128)S(1)} %shard_map.63.inverse_two, f32[1024,512]{1,0:T(8,128)S(1)} %get-tuple-element.29.outer_half), custom_call_target="tpu_custom_call" | custom-call | tf_op jit(solution)/shard_map/pallas_call | solution.py:251
  79.0 1.4 %collective-permute-done.27.theirs = f32[2,64,1024]{2,1,0:T(8,128)S(1)} collective-permute-done((f32[2,64,1024]{2,1,0:T(8,128)S(1)}, f32[2,64,1024]{2,1,0:T(8,128)S(1)}, u32[]{:S(2)}, u32[]{:S(2)}) %collective-permute-start.27) | collective-permute-done | bytes 524320 | tf_op jit(solution)/shard_map/ppermute | solution.py:21
  81.4 2.7 %shard_map.67 = f32[4,64,256]{2,1,0:T(8,128)} custom-call(s32[8,4]{1,0:T(8,128)S(1)} %copy.8.order_one.refs_0_, s32[4,6]{1,0:T(4,128)S(1)} %copy-done.3, f32[2,64,256]{2,1,0:T(8,128)S(1)} %copy-done.1, f32[2,64,256]{2,1,0:T(8,128)S(1)} %collective-permute-done.28.data_other, f32[512,256]{1,0:T(8,128)S(1)} %get-tuple-element.32.coupling_inner, ...), custom_call_target="tpu_custom_call" | custom-call | tf_op jit(solution)/shard_map/pallas_call | solution.py:251
  (58 shorter events, 18.5 us)
Async XLA Ops:
  0.6 4.9 %collective-permute-start = (f32[4,64,1024]{2,1,0:T(8,128)}, f32[4,64,1024]{2,1,0:T(8,128)S(1)}, u32[]{:S(2)}, u32[]{:S(2)}) collective-permute-start(f32[4,64,1024]{2,1,0:T(8,128)} %own.3), channel_id=1, source_target_pairs={{0,4},{4,0},{8,12},{12,8},{16,20},{20,16},{24,28},{28,24},{1,5},{5... | collective-permute-start | bytes 3145736 | tf_op jit(solution)/shard_map/ppermute | solution.py:21
  1.2 10.5 %collective-permute-start.8 = (f32[2,64,256]{2,1,0:T(8,128)}, f32[2,64,256]{2,1,0:T(8,128)S(1)}, u32[]{:S(2)}, u32[]{:S(2)}) collective-permute-start(f32[2,64,256]{2,1,0:T(8,128)} %data_own.1), channel_id=1, source_target_pairs={{0,8},{4,12},{8,0},{12,4},{16,24},{20,28},{24,16},{28,20},{1,9},{5... | collective-permute-start | bytes 393224 | tf_op jit(solution)/shard_map/ppermute | solution.py:21
  8.2 4.9 %collective-permute-start.2 = (f32[3,32,256]{2,1,0:T(8,128)S(1)}, f32[3,32,256]{2,1,0:T(8,128)S(1)}, u32[]{:S(2)}, u32[]{:S(2)}) collective-permute-start(f32[3,32,256]{2,1,0:T(8,128)S(1)} %get-tuple-element.19.refs_4_), channel_id=1, source_target_pairs={{0,1},{1,0},{2,3},{3,2},{4,5},{5,4},{6,7},{7,6},{8,9},{9,8},{10,11... | collective-permute-start | bytes 294920 | tf_op jit(solution)/shard_map/ppermute | solution.py:21
  9.7 5.8 %collective-permute-start.4 = (f32[3,32,256]{2,1,0:T(8,128)S(1)}, f32[3,32,256]{2,1,0:T(8,128)S(1)}, u32[]{:S(2)}, u32[]{:S(2)}) collective-permute-start(f32[3,32,256]{2,1,0:T(8,128)S(1)} %get-tuple-element.19.refs_4_), channel_id=1, source_target_pairs={{0,2},{1,3},{2,0},{3,1},{4,6},{5,7},{6,4},{7,5},{8,10},{9,11},{10,... | collective-permute-start | bytes 294920 | tf_op jit(solution)/shard_map/ppermute | solution.py:21
  11.2 5.5 %collective-permute-start.6 = (f32[3,32,256]{2,1,0:T(8,128)S(1)}, f32[3,32,256]{2,1,0:T(8,128)S(1)}, u32[]{:S(2)}, u32[]{:S(2)}) collective-permute-start(f32[3,32,256]{2,1,0:T(8,128)S(1)} %get-tuple-element.19.refs_4_), channel_id=1, source_target_pairs={{0,3},{1,2},{2,1},{3,0},{4,7},{5,6},{6,5},{7,4},{8,11},{9,10},{10,... | collective-permute-start | bytes 294920 | tf_op jit(solution)/shard_map/ppermute | solution.py:21
  11.7 6.8 %collective-permute-start.1 = (f32[3,32,256]{2,1,0:T(8,128)S(1)}, f32[3,32,256]{2,1,0:T(8,128)S(1)}, u32[]{:S(2)}, u32[]{:S(2)}) collective-permute-start(f32[3,32,256]{2,1,0:T(8,128)S(1)} %get-tuple-element.19.refs_4_), channel_id=1, source_target_pairs={{0,4},{4,0},{8,12},{12,8},{16,20},{20,16},{24,28},{28,24},{1,5},{5... | collective-permute-start | bytes 294920 | tf_op jit(solution)/shard_map/ppermute | solution.py:21
  13.1 5.5 %collective-permute-start.3 = (f32[3,32,256]{2,1,0:T(8,128)S(1)}, f32[3,32,256]{2,1,0:T(8,128)S(1)}, u32[]{:S(2)}, u32[]{:S(2)}) collective-permute-start(f32[3,32,256]{2,1,0:T(8,128)S(1)} %collective-permute-done.2.refs_6_), channel_id=1, source_target_pairs={{0,4},{4,0},{8,12},{12,8},{16,20},{20,16},{24,28},{28,24},{1,5},{5... | collective-permute-start | bytes 294920 | tf_op jit(solution)/shard_map/ppermute | solution.py:21
  15.5 3.1 %collective-permute-start.5 = (f32[3,32,256]{2,1,0:T(8,128)S(1)}, f32[3,32,256]{2,1,0:T(8,128)S(1)}, u32[]{:S(2)}, u32[]{:S(2)}) collective-permute-start(f32[3,32,256]{2,1,0:T(8,128)S(1)} %collective-permute-done.4.refs_8_), channel_id=1, source_target_pairs={{0,4},{4,0},{8,12},{12,8},{16,20},{20,16},{24,28},{28,24},{1,5},{5... | collective-permute-start | bytes 294920 | tf_op jit(solution)/shard_map/ppermute | solution.py:21
  16.8 17.2 %collective-permute-start.10 = (f32[6,64,256]{2,1,0:T(8,128)S(1)}, f32[6,64,256]{2,1,0:T(8,128)S(1)}, u32[]{:S(2)}, u32[]{:S(2)}) collective-permute-start(f32[6,64,256]{2,1,0:T(8,128)S(1)} %constant_dynamic-update-slice_fusion.refs_6_), channel_id=1, source_target_pairs={{0,2},{1,3},{2,0},{3,1},{4,6},{5,7},{6,4},{7,5},{8,10},{9,11},{10,... | collective-permute-start | bytes 1179656 | tf_op jit(solution)/shard_map/ppermute | solution.py:21
  22.4 9.2 %collective-permute-start.23 = (f32[2,64,512]{2,1,0:T(8,128)S(1)}, f32[2,64,512]{2,1,0:T(8,128)S(1)}, u32[]{:S(2)}, u32[]{:S(2)}) collective-permute-start(f32[2,64,512]{2,1,0:T(8,128)S(1)} %get-tuple-element.28.refs_2_), channel_id=1, source_target_pairs={{0,8},{4,12},{8,0},{12,4},{16,24},{20,28},{24,16},{28,20},{1,9},{5... | collective-permute-start | bytes 786440 | tf_op jit(solution)/shard_map/ppermute | solution.py:21
  23.5 9.6 %collective-permute-start.12 = (f32[64,512]{1,0:T(8,128)S(1)}, f32[64,512]{1,0:T(8,128)S(1)}, u32[]{:S(2)}, u32[]{:S(2)}) collective-permute-start(f32[64,512]{1,0:T(8,128)S(1)} %get-tuple-element.25), channel_id=1, source_target_pairs={{0,8},{4,12},{8,0},{12,4},{16,24},{20,28},{24,16},{28,20},{1,9},{5... | collective-permute-start | bytes 393224 | tf_op jit(solution)/shard_map/ppermute | solution.py:21
  24.5 10.8 %collective-permute-start.21 = (f32[2,64,512]{2,1,0:T(8,128)S(1)}, f32[2,64,512]{2,1,0:T(8,128)S(1)}, u32[]{:S(2)}, u32[]{:S(2)}) collective-permute-start(f32[2,64,512]{2,1,0:T(8,128)S(1)} %get-tuple-element.28.refs_2_), channel_id=1, source_target_pairs={{0,2},{1,3},{2,0},{3,1},{4,6},{5,7},{6,4},{7,5},{8,10},{9,11},{10,... | collective-permute-start | bytes 786440 | tf_op jit(solution)/shard_map/ppermute | solution.py:21
  25.3 10.7 %collective-permute-start.20 = (f32[2,64,512]{2,1,0:T(8,128)S(1)}, f32[2,64,512]{2,1,0:T(8,128)S(1)}, u32[]{:S(2)}, u32[]{:S(2)}) collective-permute-start(f32[2,64,512]{2,1,0:T(8,128)S(1)} %get-tuple-element.28.refs_2_), channel_id=1, source_target_pairs={{0,1},{1,0},{2,3},{3,2},{4,5},{5,4},{6,7},{7,6},{8,9},{9,8},{10,11... | collective-permute-start | bytes 786440 | tf_op jit(solution)/shard_map/ppermute | solution.py:21
  31.6 8.0 %collective-permute-start.25 = (f32[2,64,512]{2,1,0:T(8,128)S(1)}, f32[2,64,512]{2,1,0:T(8,128)S(1)}, u32[]{:S(2)}, u32[]{:S(2)}) collective-permute-start(f32[2,64,512]{2,1,0:T(8,128)S(1)} %collective-permute-done.23.refs_6_), channel_id=1, source_target_pairs={{0,2},{1,3},{2,0},{3,1},{4,6},{5,7},{6,4},{7,5},{8,10},{9,11},{10,... | collective-permute-start | bytes 786440 | tf_op jit(solution)/shard_map/ppermute | solution.py:21
  33.2 12.0 %collective-permute-start.9 = (f32[6,64,256]{2,1,0:T(8,128)S(1)}, f32[6,64,256]{2,1,0:T(8,128)S(1)}, u32[]{:S(2)}, u32[]{:S(2)}) collective-permute-start(f32[6,64,256]{2,1,0:T(8,128)S(1)} %constant_dynamic-update-slice_fusion.refs_6_), channel_id=1, source_target_pairs={{0,1},{1,0},{2,3},{3,2},{4,5},{5,4},{6,7},{7,6},{8,9},{9,8},{10,11... | collective-permute-start | bytes 1179656 | tf_op jit(solution)/shard_map/ppermute | solution.py:21
  33.9 26.7 %collective-permute-start.11 = (f32[6,64,256]{2,1,0:T(8,128)S(1)}, f32[6,64,256]{2,1,0:T(8,128)S(1)}, u32[]{:S(2)}, u32[]{:S(2)}) collective-permute-start(f32[6,64,256]{2,1,0:T(8,128)S(1)} %collective-permute-done.10.refs_8_), channel_id=1, source_target_pairs={{0,1},{1,0},{2,3},{3,2},{4,5},{5,4},{6,7},{7,6},{8,9},{9,8},{10,11... | collective-permute-start | bytes 1179656 | tf_op jit(solution)/shard_map/ppermute | solution.py:21
  35.2 24.0 %collective-permute-start.22 = (f32[2,64,512]{2,1,0:T(8,128)S(1)}, f32[2,64,512]{2,1,0:T(8,128)S(1)}, u32[]{:S(2)}, u32[]{:S(2)}) collective-permute-start(f32[2,64,512]{2,1,0:T(8,128)S(1)} %collective-permute-done.21.refs_4_), channel_id=1, source_target_pairs={{0,1},{1,0},{2,3},{3,2},{4,5},{5,4},{6,7},{7,6},{8,9},{9,8},{10,11... | collective-permute-start | bytes 786440 | tf_op jit(solution)/shard_map/ppermute | solution.py:21
  36.0 27.6 %collective-permute-start.24 = (f32[2,64,512]{2,1,0:T(8,128)S(1)}, f32[2,64,512]{2,1,0:T(8,128)S(1)}, u32[]{:S(2)}, u32[]{:S(2)}) collective-permute-start(f32[2,64,512]{2,1,0:T(8,128)S(1)} %collective-permute-done.20.refs_3_), channel_id=1, source_target_pairs={{0,8},{4,12},{8,0},{12,4},{16,24},{20,28},{24,16},{28,20},{1,9},{5... | collective-permute-start | bytes 786440 | tf_op jit(solution)/shard_map/ppermute | solution.py:21
  39.6 25.2 %collective-permute-start.26 = (f32[2,64,512]{2,1,0:T(8,128)S(1)}, f32[2,64,512]{2,1,0:T(8,128)S(1)}, u32[]{:S(2)}, u32[]{:S(2)}) collective-permute-start(f32[2,64,512]{2,1,0:T(8,128)S(1)} %collective-permute-done.25.refs_8_), channel_id=1, source_target_pairs={{0,1},{1,0},{2,3},{3,2},{4,5},{5,4},{6,7},{7,6},{8,9},{9,8},{10,11... | collective-permute-start | bytes 786440 | tf_op jit(solution)/shard_map/ppermute | solution.py:21
  45.2 21.8 %collective-permute-start.14 = (f32[64,512]{1,0:T(8,128)S(1)}, f32[64,512]{1,0:T(8,128)S(1)}, u32[]{:S(2)}, u32[]{:S(2)}) collective-permute-start(f32[64,512]{1,0:T(8,128)S(1)} %add.3.refs_0_), channel_id=1, source_target_pairs={{0,1},{1,0},{2,3},{3,2},{4,5},{5,4},{6,7},{7,6},{8,9},{9,8},{10,11... | collective-permute-start | bytes 393224 | tf_op jit(solution)/shard_map/ppermute | solution.py:21
  59.2 7.7 %collective-permute-start.16 = (f32[64,512]{1,0:T(8,128)S(1)}, f32[64,512]{1,0:T(8,128)S(1)}, u32[]{:S(2)}, u32[]{:S(2)}) collective-permute-start(f32[64,512]{1,0:T(8,128)S(1)} %add.3.refs_0_), channel_id=1, source_target_pairs={{0,2},{1,3},{2,0},{3,1},{4,6},{5,7},{6,4},{7,5},{8,10},{9,11},{10,... | collective-permute-start | bytes 393224 | tf_op jit(solution)/shard_map/ppermute | solution.py:21
  60.7 9.2 %collective-permute-start.18 = (f32[64,512]{1,0:T(8,128)S(1)}, f32[64,512]{1,0:T(8,128)S(1)}, u32[]{:S(2)}, u32[]{:S(2)}) collective-permute-start(f32[64,512]{1,0:T(8,128)S(1)} %add.3.refs_0_), channel_id=1, source_target_pairs={{0,3},{1,2},{2,1},{3,0},{4,7},{5,6},{6,5},{7,4},{8,11},{9,10},{10,... | collective-permute-start | bytes 393224 | tf_op jit(solution)/shard_map/ppermute | solution.py:21
  66.0 15.5 %collective-permute-start.29 = (f32[256,768]{1,0:T(8,128)S(1)}, f32[256,768]{1,0:T(8,128)S(1)}, u32[]{:S(2)}, u32[]{:S(2)}) collective-permute-start(f32[256,768]{1,0:T(8,128)S(1)} %get-tuple-element.33.driven), channel_id=1, source_target_pairs={{0,4},{4,0},{8,12},{12,8},{16,20},{20,16},{24,28},{28,24},{1,5},{5... | collective-permute-start | bytes 2359304 | tf_op jit(solution)/shard_map/ppermute | solution.py:21
  66.1 3.8 %collective-permute-start.13 = (f32[64,512]{1,0:T(8,128)S(1)}, f32[64,512]{1,0:T(8,128)S(1)}, u32[]{:S(2)}, u32[]{:S(2)}) collective-permute-start(f32[64,512]{1,0:T(8,128)S(1)} %add.3.refs_0_), channel_id=1, source_target_pairs={{0,4},{4,0},{8,12},{12,8},{16,20},{20,16},{24,28},{28,24},{1,5},{5... | collective-permute-start | bytes 393224 | tf_op jit(solution)/shard_map/ppermute | solution.py:21
  (10 other events, 20.5 us)
where the time goes:
time: 84.4 us; the launch traced here: 84.2 us
  waiting for transfers between devices  38.7 us (46%)
  starting transfers between devices  22.3 us (26%)
  Pallas kernels  18.8 us (22%)
  local copies, waits for them, and re-layouts  3.6 us (4%)
    ppermute x30, waiting for transfers between devices, swapped(): return lax.ppermute(value, axis, pairs)  38.7 us
    ppermute x30, starting transfers between devices, swapped(): return lax.ppermute(value, axis, pairs)  22.3 us
    pallas_call x9, Pallas kernels, call(): pl.pallas_call(kernel, in_specs=[smem] * scalar_count + [vmem] * (len(arg...  18.8 us
    unnamed x11, local copies, waits for them, and re-layouts  3.59 us
  transfers between devices with their start and end apart: 30, of which 13 were waited for; matrix products, arithmetic and copies ran while one was open for 2% of the time, Pallas kernels for 19%

commit v1 on v0

--- a/solution.py
+++ b/solution.py
@@ -77,7 +77,7 @@
     return jnp.where(which == tree.half, own[row_edge, rows, column], other[row_edge, rows, column])
 
 
-def first_kernel(order_one, order_two, own, other, piece, coupling, coupling_own):
+def first_kernel(order_one, order_two, own, other, data, piece, coupling, bulk):
     tree = Tree(order_one, order_two)
     half_width = piece.shape[1]
     width = coupling.shape[1]
@@ -94,8 +94,22 @@
     for slot in range(4):
         which, edge = tree.edge(slot)
         coupling[slot] = block_of(tree, own, other, which, edge, 0, width, tree.inner(which))
-    for slot in range(2):
-        coupling_own[slot] = coupling[2 * tree.half + slot]
+    same, inner_leaf, outer_leaf = packing(tree, tree.node)
+    holder = jnp.where(outer_leaf[0] == inner_leaf[0], 0, 1)
+    for slot in range(2):
+        bulk[slot] = data[slot]
+        bulk[2 + slot] = coupling[2 * tree.half + slot]
+        row = jnp.where(same, holder, slot)
+        column = jnp.where(same, slot, jnp.where(outer_leaf[slot] == inner_leaf[0], 0, 1))
+        which, edge = tree.edge(2 * tree.half + row)
+        _, column_edge = tree.edge(4 + column)
+        bulk[4 + slot] = block_of(tree, own, other, which, edge, 0, width, column_edge)
+
+
+def packing(tree, node):
+    inner_leaf = [tree.order_two[node, 4 + slot] // 3 for slot in range(2)]
+    outer_leaf = [tree.order_two[node, 2 * tree.half + slot] // 3 for slot in range(2)]
+    return inner_leaf[0] == inner_leaf[1], inner_leaf, outer_leaf
 
 
 def interface_rows(tree, own, other, position, start, size):
@@ -109,7 +123,8 @@
 
 
 def second_kernel(count, order_one, order_two, own, other, *refs):
-    pieces, (inner_rows, inverse_out, coupling_inner, right_out, sums) = refs[: 2 * count], refs[2 * count :]
+    pieces, outs = refs[: 2 * count], refs[2 * count :]
+    inner_rows, inverse_out, coupling_inner, right_out, right_half, sums = outs
     tree = Tree(order_one, order_two)
     half_width = pieces[0].shape[1]
     width = 2 * half_width
@@ -125,6 +140,7 @@
     inverse_out[...] = inverse
     right = product(inverse, coupling_inner[...], NT)
     right_out[...] = right
+    right_half[...] = right_out[pl.ds(pl.multiple_of(tree.half * (W // 2), W // 2), W // 2), :]
     start = pl.multiple_of(tree.half * half_width, half_width)
     left = jnp.concatenate([pieces[0][1], pieces[0][2]], axis=0)
     change = product(left, right)
@@ -133,15 +149,13 @@
         inner_rows[rows, :] = interface_rows(tree, own, other, 4 + slot, start, half_width) - change[rows]
 
 
-def outer_kernel(order_one, order_two, own, other, coupling, right, outer_all, outer_own):
+def outer_kernel(order_one, order_two, own, other, coupling, right, outer_all):
     tree = Tree(order_one, order_two)
     width = coupling.shape[1]
     change = product(coupling[...].reshape(4 * width, W), right[...])
     for slot in range(4):
         base = interface_rows(tree, own, other, slot, 0, width)
         outer_all[slot] = base - change[slot * width : (slot + 1) * width]
-    for slot in range(2):
-        outer_own[slot] = outer_all[2 * tree.half + slot]
 
 
 def third_kernel(count, *refs):
@@ -159,19 +173,38 @@
     inverse_out[...] = newton(sums[...])
 
 
-def near_kernel(count, order_one, order_two, own, other, coupling, inverse_one, *refs):
-    bulks, (base_out, driven_one, coupling_half, data_half) = refs[:count], refs[count:]
-    tree = Tree(order_one, order_two)
-    node_bit = tree.node % 2
-    width = own.shape[1]
-    for mask in range(count):
+def gathered(tree, bulks, data_half, coupling_half, packed_zero, packed_one):
+    width = bulks[0].shape[1]
+    for mask, bulk in enumerate(bulks):
         at = (tree.member ^ mask) * width
         for slot in range(2):
-            row = pl.multiple_of(slot * W + at, width)
-            coupling_half[pl.ds(row, width), :] = bulks[mask][4 + slot]
-            for far in range(2):
-                row = pl.multiple_of((2 * (node_bit ^ far) + slot) * W + at, width)
-                data_half[pl.ds(row, width), :] = bulks[mask][2 * far + slot]
+            target = pl.ds(pl.multiple_of(slot * W + at, width), width)
+            data_half[target, :] = bulk[slot]
+            coupling_half[target, :] = bulk[2 + slot]
+        target = pl.ds(pl.multiple_of(at, width), width)
+        packed_zero[target, :] = bulk[4]
+        packed_one[target, :] = bulk[5]
+
+
+def outer_rows(tree, node, coupling_split, packed_zero, packed_one, right, outer_half):
+    same, inner_leaf, outer_leaf = packing(tree, node)
+    packed = (packed_zero, packed_one)
+    change = product(coupling_split, right)
+    for slot in range(2):
+        rows = slice(slot * W, (slot + 1) * W)
+        for column in range(2):
+            columns = slice(column * W, (column + 1) * W)
+            value = jnp.where(same, packed[column][...], packed[slot][...])
+            value = jnp.where(outer_leaf[slot] == inner_leaf[column], value, 0.0)
+            outer_half[rows, columns] = value - change[rows, columns]
+
+
+def near_kernel(count, order_one, order_two, own, other, coupling, inverse_one, right, *refs):
+    bulks, outs = refs[:count], refs[count:]
+    base_out, outer_half, driven, coupling_half, data_half, packed_zero, packed_one = outs
+    tree = Tree(order_one, order_two)
+    width = own.shape[1]
+    gathered(tree, bulks, data_half, coupling_half, packed_zero, packed_one)
     coupling_split = parts_of(coupling_half[...])
     scaled = product(coupling[...].reshape(4 * width, W), inverse_one[...])
     local = product(scaled, coupling_split, NT)
@@ -183,34 +216,36 @@
             value = jnp.where(which == column_which, value, 0.0)
             rows, columns = slice(slot * width, (slot + 1) * width), slice(column * W, (column + 1) * W)
             base_out[slot, :, columns] = value - local[rows, columns]
-    near = data_half[pl.ds(pl.multiple_of(node_bit * 2 * W, W), 2 * W), :]
-    driven_one[...] = product(near.T, coupling_split)
-
-
-def far_kernel(count, data_half, driven_one, *refs):
-    outers, (driven, outer_half) = refs[: 2 * count], refs[2 * count :]
-    node_bit, member = (lax.axis_index("leaf") // 2) % 2, lax.axis_index("sub")
-    width = outers[0].shape[1]
-    for mask in range(count):
-        at = (member ^ mask) * width
-        for slot in range(2):
-            for far in range(2):
-                row = pl.multiple_of((2 * (node_bit ^ far) + slot) * W + at, width)
-                outer_half[pl.ds(row, width), :] = outers[mask + far * count][slot]
-    driven[:, : 2 * W] = product(data_half[...].T, outer_half[...])
-    driven[:, 2 * W :] = driven_one[...]
-
-
-def top_kernel(base, outer_all, inverse_two, outer_half, mine, theirs):
-    half, node_bit = lax.axis_index("leaf") % 2, (lax.axis_index("leaf") // 2) % 2
+    outer_rows(tree, tree.node, coupling_split, packed_zero, packed_one, right[...], outer_half)
+    turned = parts_of(data_half[...].T)
+    driven[:, : 2 * W] = product(turned, outer_half[...])
+    driven[:, 2 * W :] = product(turned, coupling_split)
+
+
+def far_kernel(count, order_one, order_two, driven_near, right_mine, right_other, *refs):
+    bulks, outs = refs[:count], refs[count:]
+    outer_half, driven, coupling_half, data_half, packed_zero, packed_one, right = outs
+    tree = Tree(order_one, order_two)
+    gathered(tree, bulks, data_half, coupling_half, packed_zero, packed_one)
+    for side, held in enumerate((right_mine, right_other)):
+        right[pl.ds(pl.multiple_of((tree.half ^ side) * (W // 2), W // 2), W // 2), :] = held[...]
+    node = tree.node ^ 1
+    outer_rows(tree, node, parts_of(coupling_half[...]), packed_zero, packed_one, right[...], outer_half)
+    driven[:, : 2 * W] = driven_near[:, : 2 * W] + product(data_half[...].T, outer_half[...])
+    driven[:, 2 * W :] = driven_near[:, 2 * W :]
+
+
+def top_kernel(base, outer_all, inverse_two, outer_near, outer_far, mine, theirs):
+    half = lax.axis_index("leaf") % 2
     slots, width, columns = base.shape
-    scaled = product(outer_all[...].reshape(slots * width, columns), inverse_two[...])
-    change = -product(scaled, outer_half[...], NT)
-    for bit in range(2):
-        held = jnp.where(bit == node_bit, base[...], 0.0)
-        part = held + change[:, bit * columns : (bit + 1) * columns].reshape(slots, width, columns)
-        mine[:, :, bit * columns : (bit + 1) * columns] = jnp.where(half == 0, part[:2], part[2:])
-        theirs[:, :, bit * columns : (bit + 1) * columns] = jnp.where(half == 0, part[2:], part[:2])
+    scaled = parts_of(product(outer_all[...].reshape(slots * width, columns), inverse_two[...]))
+    for far, outer in enumerate((outer_near, outer_far)):
+        part = -product(scaled, outer[...], NT).reshape(slots, width, columns)
+        if not far:
+            part = base[...] + part
+        target = slice(far * columns, (far + 1) * columns)
+        mine[:, :, target] = jnp.where(half == 0, part[:2], part[2:])
+        theirs[:, :, target] = jnp.where(half == 0, part[2:], part[:2])
 
 
 def leaf_kernel(order_one, order_two, data_own, data_other, coupling_inner, inverse_one, inverse_two, driven, driven_other, leaf_data, inner):
@@ -236,12 +271,12 @@
 
 
 def join_kernel(mine, theirs, top_map):
-    half = lax.axis_index("leaf") % 2
+    half, node_bit = lax.axis_index("leaf") % 2, (lax.axis_index("leaf") // 2) % 2
     columns = mine.shape[2] // 2
-    for bit in range(2):
-        source = slice(bit * columns, (bit + 1) * columns)
+    for far in range(2):
+        source = slice(far * columns, (far + 1) * columns)
         for side, held in enumerate((mine, theirs)):
-            target = pl.multiple_of((2 * bit + (half ^ side)) * columns, columns)
+            target = pl.multiple_of((2 * (node_bit ^ far) + (half ^ side)) * columns, columns)
             top_map[:, :, pl.ds(target, columns)] = held[:, :, source]
 
 
@@ -283,36 +318,38 @@
         return [item for value in values for item in (value, swapped(value, "leaf", 1))]
 
     other = swapped(leaf_maps, "leaf", 1)
-    data_far = swapped(top_data, "leaf", 2)
-    piece, coupling, coupling_own = call(
-        first_kernel, 2, [(3, half_width, W), (4, width, W), (2, width, W)], [], *orders, leaf_maps, other
+    piece, coupling, bulk = call(
+        first_kernel, 2, [(3, half_width, W), (4, width, W), (6, width, W)], [],
+        *orders, leaf_maps, other, top_data,
     )
     pieces = with_sibling(across(piece))
     data_other = swapped(top_data, "leaf", 1)
-    bulks = spread(jnp.concatenate([top_data, data_far, coupling_own], axis=0), bits[:-1])
-    inner_rows, inverse_one, coupling_inner, right = call(
+    bulks = spread(bulk, bits)
+    inner_rows, inverse_one, coupling_inner, right, right_half = call(
         lambda *refs: second_kernel(count, *refs), 2,
-        [(2 * half_width, 2 * W), (W, W), (2 * W, W), (W, 2 * W)], [(W, W)],
+        [(2 * half_width, 2 * W), (W, W), (2 * W, W), (W, 2 * W), (W // 2, 2 * W)], [(W, W)],
         *orders, leaf_maps, other, *pieces,
     )
     summed = inner_rows + swapped(inner_rows, "leaf", 2)
-    outer_all, outer_own = call(
-        outer_kernel, 2, [(4, width, 2 * W), (2, width, 2 * W)], [], *orders, leaf_maps, other, coupling, right
-    )
-    outers = spread(outer_own, bits)
+    right_mine = swapped(right_half, "leaf", 2)
+    right_other = swapped(right_mine, "leaf", 1)
+    (outer_all,) = call(outer_kernel, 2, [(4, width, 2 * W)], [], *orders, leaf_maps, other, coupling, right)
     (inverse_two,) = call(
         lambda *refs: third_kernel(count, *refs), 0, [(2 * W, 2 * W)], [(2 * W, 2 * W)],
         *with_sibling(across(summed)),
     )
-    base, driven_one, _, data_half = call(
+    scratch = [(2 * W, W), (2 * W, K), (W, W), (W, W)]
+    base, outer_near, driven_near = call(
         lambda *refs: near_kernel(count, *refs), 2,
-        [(4, width, 2 * W), (K, W), (2 * W, W), (4 * W, K)], [], *orders, leaf_maps, other, coupling, inverse_one, *bulks,
-    )
-    driven, outer_half = call(
-        lambda *refs: far_kernel(count, *refs), 0, [(K, 3 * W), (4 * W, 2 * W)], [], data_half, driven_one, *outers
+        [(4, width, 2 * W), (2 * W, 2 * W), (K, 3 * W)], scratch,
+        *orders, leaf_maps, other, coupling, inverse_one, right, *bulks[:count],
+    )
+    outer_far, driven = call(
+        lambda *refs: far_kernel(count, *refs), 2, [(2 * W, 2 * W), (K, 3 * W)], scratch + [(W, 2 * W)],
+        *orders, driven_near, right_mine, right_other, *bulks[count:],
     )
     driven_other = swapped(driven, "leaf", 1)
-    mine, theirs = call(top_kernel, 0, [(2, width, 4 * W)] * 2, [], base, outer_all, inverse_two, outer_half)
+    mine, theirs = call(top_kernel, 0, [(2, width, 4 * W)] * 2, [], base, outer_all, inverse_two, outer_near, outer_far)
     received = swapped(theirs, "leaf", 1)
     (leaf_data,) = call(
         leaf_kernel, 2, [(4, width, K)], [(2 * width, K)],

time: 84.4 us -> 75.5 us (0.89)
  waiting for transfers between devices: 38.7 us -> 30.7 us
  starting transfers between devices: 22.3 us -> 20.9 us
  Pallas kernels: 18.8 us -> 20.1 us
    ppermute x30 -> x28, waiting for transfers between devices: 38.7 us -> 30.7 us  [swapped(): return lax.ppermute(value, axis, pairs)]
    ppermute x30 -> x28, starting transfers between devices: 22.3 us -> 20.9 us  [swapped(): return lax.ppermute(value, axis, pairs)]
    pallas_call x9, Pallas kernels: 18.8 us -> 20.1 us  [call(): pl.pallas_call(kernel, in_specs=[smem] * scalar_count + [vmem] * (len(arg...]
  transfers between devices with their start and end apart: 30 -> 28, of which waited for: 13 -> 13; matrix products, arithmetic and copies ran while one was open for 2% -> 1% of each run, Pallas kernels for 19% -> 22%
where the time goes in v1:
time: 75.5 us; the launch traced here: 75.3 us
  waiting for transfers between devices  30.7 us (41%)
  starting transfers between devices  20.9 us (28%)
  Pallas kernels  20.1 us (27%)
  local copies, waits for them, and re-layouts  2.9 us (4%)
  between operations  0.76 us (1%)
    ppermute x28, waiting for transfers between devices, swapped(): return lax.ppermute(value, axis, pairs)  30.7 us
    ppermute x28, starting transfers between devices, swapped(): return lax.ppermute(value, axis, pairs)  20.9 us
    pallas_call x9, Pallas kernels, call(): pl.pallas_call(kernel, in_specs=[smem] * scalar_count + [vmem] * (len(arg...  20.1 us
    unnamed x11, local copies, waits for them, and re-layouts  2.9 us
  transfers between devices with their start and end apart: 28, of which 13 were waited for; matrix products, arithmetic and copies ran while one was open for 1% of the time, Pallas kernels for 22%

profile of v1, /device:TPU:0, one launch (start us, length us, event | category | flops | bytes accessed | tf_op | source)
XLA Modules:
  0.0 75.3 jit_solution(13117119291881403823)
XLA Ops:
  2.0 1.7 %collective-permute-done.other.refs_3_ = f32[4,64,1024]{2,1,0:T(8,128)S(1)} collective-permute-done((f32[4,64,1024]{2,1,0:T(8,128)}, f32[4,64,1024]{2,1,0:T(8,128)S(1)}, u32[]{:S(2)}, u32[]{:S(2)}) %collective-permute-start) | collective-permute-done | bytes 1048608 | tf_op jit(solution)/shard_map/ppermute | solution.py:21
  3.7 1.2 %copy-done = f32[4,64,1024]{2,1,0:T(8,128)S(1)} copy-done((f32[4,64,1024]{2,1,0:T(8,128)S(1)}, f32[4,64,1024]{2,1,0:T(8,128)}, u32[]{:S(2)}) %copy-start) | copy-done | bytes 1048600
  4.9 0.9 %copy-done.2 = f32[2,64,256]{2,1,0:T(8,128)S(1)} copy-done((f32[2,64,256]{2,1,0:T(8,128)S(1)}, f32[2,64,256]{2,1,0:T(8,128)}, u32[]{:S(2)}) %copy-start.2) | copy-done | bytes 131096
  6.7 3.0 %collective-permute-start.21 = (f32[6,64,256]{2,1,0:T(8,128)S(1)}, f32[6,64,256]{2,1,0:T(8,128)S(1)}, u32[]{:S(2)}, u32[]{:S(2)}) collective-permute-start(f32[6,64,256]{2,1,0:T(8,128)S(1)} %get-tuple-element.21.refs_7_), channel_id=1, source_target_pairs={{0,8},{4,12},{8,0},{12,4},{16,24},{20,28},{24,16},{28,20},{1,9},{5... | collective-permute-start | bytes 1179656 | tf_op jit(solution)/shard_map/ppermute | solution.py:21
  9.7 1.5 %collective-permute-start.2 = (f32[3,32,256]{2,1,0:T(8,128)S(1)}, f32[3,32,256]{2,1,0:T(8,128)S(1)}, u32[]{:S(2)}, u32[]{:S(2)}) collective-permute-start(f32[3,32,256]{2,1,0:T(8,128)S(1)} %get-tuple-element.18.refs_4_), channel_id=1, source_target_pairs={{0,1},{1,0},{2,3},{3,2},{4,5},{5,4},{6,7},{7,6},{8,9},{9,8},{10,11... | collective-permute-start | bytes 294920 | tf_op jit(solution)/shard_map/ppermute | solution.py:21
  11.1 1.5 %collective-permute-start.4 = (f32[3,32,256]{2,1,0:T(8,128)S(1)}, f32[3,32,256]{2,1,0:T(8,128)S(1)}, u32[]{:S(2)}, u32[]{:S(2)}) collective-permute-start(f32[3,32,256]{2,1,0:T(8,128)S(1)} %get-tuple-element.18.refs_4_), channel_id=1, source_target_pairs={{0,2},{1,3},{2,0},{3,1},{4,6},{5,7},{6,4},{7,5},{8,10},{9,11},{10,... | collective-permute-start | bytes 294920 | tf_op jit(solution)/shard_map/ppermute | solution.py:21
  13.7 5.4 %collective-permute-done.21.refs_5_ = f32[6,64,256]{2,1,0:T(8,128)S(1)} collective-permute-done((f32[6,64,256]{2,1,0:T(8,128)S(1)}, f32[6,64,256]{2,1,0:T(8,128)S(1)}, u32[]{:S(2)}, u32[]{:S(2)}) %collective-permute-start.21) | collective-permute-done | bytes 393248 | tf_op jit(solution)/shard_map/ppermute | solution.py:21
  19.1 1.7 %collective-permute-start.23 = (f32[6,64,256]{2,1,0:T(8,128)S(1)}, f32[6,64,256]{2,1,0:T(8,128)S(1)}, u32[]{:S(2)}, u32[]{:S(2)}) collective-permute-start(f32[6,64,256]{2,1,0:T(8,128)S(1)} %collective-permute-done.21.refs_5_), channel_id=1, source_target_pairs={{0,2},{1,3},{2,0},{3,1},{4,6},{5,7},{6,4},{7,5},{8,10},{9,11},{10,... | collective-permute-start | bytes 1179656 | tf_op jit(solution)/shard_map/ppermute | solution.py:21
  20.8 1.4 %collective-permute-start.6 = (f32[3,32,256]{2,1,0:T(8,128)S(1)}, f32[3,32,256]{2,1,0:T(8,128)S(1)}, u32[]{:S(2)}, u32[]{:S(2)}) collective-permute-start(f32[3,32,256]{2,1,0:T(8,128)S(1)} %get-tuple-element.18.refs_4_), channel_id=1, source_target_pairs={{0,3},{1,2},{2,1},{3,0},{4,7},{5,6},{6,5},{7,4},{8,11},{9,10},{10,... | collective-permute-start | bytes 294920 | tf_op jit(solution)/shard_map/ppermute | solution.py:21
  22.2 4.8 %collective-permute-done.6.refs_10_ = f32[3,32,256]{2,1,0:T(8,128)S(1)} collective-permute-done((f32[3,32,256]{2,1,0:T(8,128)S(1)}, f32[3,32,256]{2,1,0:T(8,128)S(1)}, u32[]{:S(2)}, u32[]{:S(2)}) %collective-permute-start.6) | collective-permute-done | bytes 98336 | tf_op jit(solution)/shard_map/ppermute | solution.py:21
  28.5 2.8 %shard_map.60 = (f32[64,512]{1,0:T(8,128)S(1)}, f32[256,256]{1,0:T(8,128)S(1)}, f32[512,256]{1,0:T(8,128)S(1)}, f32[256,512]{1,0:T(8,128)S(1)}, f32[128,512]{1,0:T(8,128)S(1)}) custom-call(s32[8,4]{1,0:T(8,128)S(1)} %copy.8.order_one.refs_0_, s32[4,6]{1,0:T(4,128)S(1)} %copy-done.4, f32[4,64,1024]{2,1,0:T(8,128)S(1)} %copy-done, ...), custom_call_target="tpu_custom_call" | custom-call | tf_op jit(solution)/shard_map/pallas_call | solution.py:286
  32.2 1.6 %collective-permute-start.10 = (f32[6,64,256]{2,1,0:T(8,128)S(1)}, f32[6,64,256]{2,1,0:T(8,128)S(1)}, u32[]{:S(2)}, u32[]{:S(2)}) collective-permute-start(f32[6,64,256]{2,1,0:T(8,128)S(1)} %collective-permute-done.9.refs_9_), channel_id=1, source_target_pairs={{0,1},{1,0},{2,3},{3,2},{4,5},{5,4},{6,7},{7,6},{8,9},{9,8},{10,11... | collective-permute-start | bytes 1179656 | tf_op jit(solution)/shard_map/ppermute | solution.py:21
  35.6 4.9 %collective-permute-done.19.refs_3_ = f32[128,512]{1,0:T(8,128)S(1)} collective-permute-done((f32[128,512]{1,0:T(8,128)S(1)}, f32[128,512]{1,0:T(8,128)S(1)}, u32[]{:S(2)}, u32[]{:S(2)}) %collective-permute-start.19) | collective-permute-done | bytes 262176 | tf_op jit(solution)/shard_map/ppermute | solution.py:21
  41.3 9.8 %collective-permute-done.11 = f32[64,512]{1,0:T(8,128)S(1)} collective-permute-done((f32[64,512]{1,0:T(8,128)S(1)}, f32[64,512]{1,0:T(8,128)S(1)}, u32[]{:S(2)}, u32[]{:S(2)}) %collective-permute-start.11) | collective-permute-done | bytes 131104 | tf_op jit(solution)/shard_map/ppermute | solution.py:21
  51.1 1.0 %collective-permute-start.13 = (f32[64,512]{1,0:T(8,128)S(1)}, f32[64,512]{1,0:T(8,128)S(1)}, u32[]{:S(2)}, u32[]{:S(2)}) collective-permute-start(f32[64,512]{1,0:T(8,128)S(1)} %add.3.refs_0_), channel_id=1, source_target_pairs={{0,1},{1,0},{2,3},{3,2},{4,5},{5,4},{6,7},{7,6},{8,9},{9,8},{10,11... | collective-permute-start | bytes 393224 | tf_op jit(solution)/shard_map/ppermute | solution.py:21
  52.6 2.1 %collective-permute-start.17 = (f32[64,512]{1,0:T(8,128)S(1)}, f32[64,512]{1,0:T(8,128)S(1)}, u32[]{:S(2)}, u32[]{:S(2)}) collective-permute-start(f32[64,512]{1,0:T(8,128)S(1)} %add.3.refs_0_), channel_id=1, source_target_pairs={{0,3},{1,2},{2,1},{3,0},{4,7},{5,6},{6,5},{7,4},{8,11},{9,10},{10,... | collective-permute-start | bytes 393224 | tf_op jit(solution)/shard_map/ppermute | solution.py:21
  54.7 2.5 %shard_map.61 = (f32[4,64,512]{2,1,0:T(8,128)S(1)}, f32[512,512]{1,0:T(8,128)S(1)}, f32[256,768]{1,0:T(8,128)S(1)}) custom-call(s32[8,4]{1,0:T(8,128)S(1)} %copy.8.order_one.refs_0_, s32[4,6]{1,0:T(4,128)S(1)} %copy-done.4, f32[4,64,1024]{2,1,0:T(8,128)S(1)} %copy-done, f32[4,64,1024]{2,1,0:T(8,128)S(1)} %collective-permute-done.other.refs_3_, ...), custom_call_target="tpu_custom_call" | custom-call | tf_op jit(solution)/shard_map/pallas_call | solution.py:286
  57.3 1.9 %shard_map.64 = (f32[512,512]{1,0:T(8,128)S(1)}, f32[256,768]{1,0:T(8,128)S(1)}) custom-call(s32[8,4]{1,0:T(8,128)S(1)} %copy.8.order_one.refs_0_, s32[4,6]{1,0:T(4,128)S(1)} %copy-done.4, f32[256,768]{1,0:T(8,128)S(1)} %get-tuple-element.25.refs_2_, f32[128,512]{1,0:T(8,128)S(1)} %collective-permute-done.19.refs_3_, ...), custom_call_target="tpu_custom_call" | custom-call | tf_op jit(solution)/shard_map/pallas_call | solution.py:286
  60.3 1.0 %shard_map.62.outer_all = f32[4,64,512]{2,1,0:T(8,128)S(1)} custom-call(s32[8,4]{1,0:T(8,128)S(1)} %copy.8.order_one.refs_0_, s32[4,6]{1,0:T(4,128)S(1)} %copy-done.4, f32[4,64,1024]{2,1,0:T(8,128)S(1)} %copy-done.1, f32[4,64,1024]{2,1,0:T(8,128)S(1)} %collective-permute-done.other.refs_3_, f32[4,64,256]{2,1,0:T(8,128)S(1)} %get-tuple-element.17.refs_4_.coupling, ...), custom_call_target="tpu_custom_call" | custom-call | tf_op jit(solution)/shard_map/pallas_call | solution.py:286
  62.2 5.7 %shard_map.63.inverse_two = f32[512,512]{1,0:T(8,128)S(1)} custom-call(f32[64,512]{1,0:T(8,128)S(1)} %add.3.refs_0_, f32[64,512]{1,0:T(8,128)S(1)} %collective-permute-done.12.refs_1_, f32[64,512]{1,0:T(8,128)S(1)} %collective-permute-done.13.refs_2_, f32[64,512]{1,0:T(8,128)S(1)} %collective-permute-done.14.refs_3_, ...), custom_call_target="tpu_custom_call" | custom-call | tf_op jit(solution)/shard_map/pallas_call | solution.py:286
  67.9 1.6 %shard_map.65 = (f32[2,64,1024]{2,1,0:T(8,128)S(1)}, f32[2,64,1024]{2,1,0:T(8,128)S(1)}) custom-call(f32[4,64,512]{2,1,0:T(8,128)S(1)} %get-tuple-element.22.base, f32[4,64,512]{2,1,0:T(8,128)S(1)} %shard_map.62.outer_all, f32[512,512]{1,0:T(8,128)S(1)} %shard_map.63.inverse_two, f32[512,512]{1,0:T(8,128)S(1)} %get-tuple-element.24.outer_near, ...), custom_call_target="tpu_custom_call" | custom-call | tf_op jit(solution)/shard_map/pallas_call | solution.py:286
  70.1 1.4 %collective-permute-done.25.theirs = f32[2,64,1024]{2,1,0:T(8,128)S(1)} collective-permute-done((f32[2,64,1024]{2,1,0:T(8,128)S(1)}, f32[2,64,1024]{2,1,0:T(8,128)S(1)}, u32[]{:S(2)}, u32[]{:S(2)}) %collective-permute-start.25) | collective-permute-done | bytes 524320 | tf_op jit(solution)/shard_map/ppermute | solution.py:21
  71.5 1.1 %shard_map.66 = f32[2,64,2048]{2,1,0:T(8,128)} custom-call(f32[2,64,1024]{2,1,0:T(8,128)S(1)} %get-tuple-element.28.mine, f32[2,64,1024]{2,1,0:T(8,128)S(1)} %collective-permute-done.25.theirs), custom_call_target="tpu_custom_call" | custom-call | tf_op jit(solution)/shard_map/pallas_call | solution.py:286
  72.6 2.8 %shard_map.67 = f32[4,64,256]{2,1,0:T(8,128)} custom-call(s32[8,4]{1,0:T(8,128)S(1)} %copy.8.order_one.refs_0_, s32[4,6]{1,0:T(4,128)S(1)} %copy-done.4, f32[2,64,256]{2,1,0:T(8,128)S(1)} %copy-done.3, f32[2,64,256]{2,1,0:T(8,128)S(1)} %collective-permute-done.26.data_other, f32[512,256]{1,0:T(8,128)S(1)} %get-tuple-element.30.coupling_inner, ...), custom_call_target="tpu_custom_call" | custom-call | tf_op jit(solution)/shard_map/pallas_call | solution.py:286
  (53 shorter events, 11.4 us)
Async XLA Ops:
  0.6 3.1 %collective-permute-start = (f32[4,64,1024]{2,1,0:T(8,128)}, f32[4,64,1024]{2,1,0:T(8,128)S(1)}, u32[]{:S(2)}, u32[]{:S(2)}) collective-permute-start(f32[4,64,1024]{2,1,0:T(8,128)} %own.3), channel_id=1, source_target_pairs={{0,4},{4,0},{8,12},{12,8},{16,20},{20,16},{24,28},{28,24},{1,5},{5... | collective-permute-start | bytes 3145736 | tf_op jit(solution)/shard_map/ppermute | solution.py:21
  6.7 12.4 %collective-permute-start.21 = (f32[6,64,256]{2,1,0:T(8,128)S(1)}, f32[6,64,256]{2,1,0:T(8,128)S(1)}, u32[]{:S(2)}, u32[]{:S(2)}) collective-permute-start(f32[6,64,256]{2,1,0:T(8,128)S(1)} %get-tuple-element.21.refs_7_), channel_id=1, source_target_pairs={{0,8},{4,12},{8,0},{12,4},{16,24},{20,28},{24,16},{28,20},{1,9},{5... | collective-permute-start | bytes 1179656 | tf_op jit(solution)/shard_map/ppermute | solution.py:21
  9.7 3.5 %collective-permute-start.1 = (f32[3,32,256]{2,1,0:T(8,128)S(1)}, f32[3,32,256]{2,1,0:T(8,128)S(1)}, u32[]{:S(2)}, u32[]{:S(2)}) collective-permute-start(f32[3,32,256]{2,1,0:T(8,128)S(1)} %get-tuple-element.18.refs_4_), channel_id=1, source_target_pairs={{0,4},{4,0},{8,12},{12,8},{16,20},{20,16},{24,28},{28,24},{1,5},{5... | collective-permute-start | bytes 294920 | tf_op jit(solution)/shard_map/ppermute | solution.py:21
  9.7 11.1 %collective-permute-start.2 = (f32[3,32,256]{2,1,0:T(8,128)S(1)}, f32[3,32,256]{2,1,0:T(8,128)S(1)}, u32[]{:S(2)}, u32[]{:S(2)}) collective-permute-start(f32[3,32,256]{2,1,0:T(8,128)S(1)} %get-tuple-element.18.refs_4_), channel_id=1, source_target_pairs={{0,1},{1,0},{2,3},{3,2},{4,5},{5,4},{6,7},{7,6},{8,9},{9,8},{10,11... | collective-permute-start | bytes 294920 | tf_op jit(solution)/shard_map/ppermute | solution.py:21
  11.1 11.0 %collective-permute-start.4 = (f32[3,32,256]{2,1,0:T(8,128)S(1)}, f32[3,32,256]{2,1,0:T(8,128)S(1)}, u32[]{:S(2)}, u32[]{:S(2)}) collective-permute-start(f32[3,32,256]{2,1,0:T(8,128)S(1)} %get-tuple-element.18.refs_4_), channel_id=1, source_target_pairs={{0,2},{1,3},{2,0},{3,1},{4,6},{5,7},{6,4},{7,5},{8,10},{9,11},{10,... | collective-permute-start | bytes 294920 | tf_op jit(solution)/shard_map/ppermute | solution.py:21
  12.7 19.5 %collective-permute-start.9 = (f32[6,64,256]{2,1,0:T(8,128)S(1)}, f32[6,64,256]{2,1,0:T(8,128)S(1)}, u32[]{:S(2)}, u32[]{:S(2)}) collective-permute-start(f32[6,64,256]{2,1,0:T(8,128)S(1)} %get-tuple-element.21.refs_7_), channel_id=1, source_target_pairs={{0,2},{1,3},{2,0},{3,1},{4,6},{5,7},{6,4},{7,5},{8,10},{9,11},{10,... | collective-permute-start | bytes 1179656 | tf_op jit(solution)/shard_map/ppermute | solution.py:21
  13.2 20.6 %collective-permute-start.8 = (f32[6,64,256]{2,1,0:T(8,128)S(1)}, f32[6,64,256]{2,1,0:T(8,128)S(1)}, u32[]{:S(2)}, u32[]{:S(2)}) collective-permute-start(f32[6,64,256]{2,1,0:T(8,128)S(1)} %get-tuple-element.21.refs_7_), channel_id=1, source_target_pairs={{0,1},{1,0},{2,3},{3,2},{4,5},{5,4},{6,7},{7,6},{8,9},{9,8},{10,11... | collective-permute-start | bytes 1179656 | tf_op jit(solution)/shard_map/ppermute | solution.py:21
  19.1 16.0 %collective-permute-start.23 = (f32[6,64,256]{2,1,0:T(8,128)S(1)}, f32[6,64,256]{2,1,0:T(8,128)S(1)}, u32[]{:S(2)}, u32[]{:S(2)}) collective-permute-start(f32[6,64,256]{2,1,0:T(8,128)S(1)} %collective-permute-done.21.refs_5_), channel_id=1, source_target_pairs={{0,2},{1,3},{2,0},{3,1},{4,6},{5,7},{6,4},{7,5},{8,10},{9,11},{10,... | collective-permute-start | bytes 1179656 | tf_op jit(solution)/shard_map/ppermute | solution.py:21
  20.8 6.3 %collective-permute-start.6 = (f32[3,32,256]{2,1,0:T(8,128)S(1)}, f32[3,32,256]{2,1,0:T(8,128)S(1)}, u32[]{:S(2)}, u32[]{:S(2)}) collective-permute-start(f32[3,32,256]{2,1,0:T(8,128)S(1)} %get-tuple-element.18.refs_4_), channel_id=1, source_target_pairs={{0,3},{1,2},{2,1},{3,0},{4,7},{5,6},{6,5},{7,4},{8,11},{9,10},{10,... | collective-permute-start | bytes 294920 | tf_op jit(solution)/shard_map/ppermute | solution.py:21
  22.2 4.8 %collective-permute-start.3 = (f32[3,32,256]{2,1,0:T(8,128)S(1)}, f32[3,32,256]{2,1,0:T(8,128)S(1)}, u32[]{:S(2)}, u32[]{:S(2)}) collective-permute-start(f32[3,32,256]{2,1,0:T(8,128)S(1)} %collective-permute-done.2.refs_6_), channel_id=1, source_target_pairs={{0,4},{4,0},{8,12},{12,8},{16,20},{20,16},{24,28},{28,24},{1,5},{5... | collective-permute-start | bytes 294920 | tf_op jit(solution)/shard_map/ppermute | solution.py:21
  31.3 9.2 %collective-permute-start.19 = (f32[128,512]{1,0:T(8,128)S(1)}, f32[128,512]{1,0:T(8,128)S(1)}, u32[]{:S(2)}, u32[]{:S(2)}) collective-permute-start(f32[128,512]{1,0:T(8,128)S(1)} %get-tuple-element.26), channel_id=1, source_target_pairs={{0,8},{4,12},{8,0},{12,4},{16,24},{20,28},{24,16},{28,20},{1,9},{5... | collective-permute-start | bytes 786440 | tf_op jit(solution)/shard_map/ppermute | solution.py:21
  32.2 20.5 %collective-permute-start.10 = (f32[6,64,256]{2,1,0:T(8,128)S(1)}, f32[6,64,256]{2,1,0:T(8,128)S(1)}, u32[]{:S(2)}, u32[]{:S(2)}) collective-permute-start(f32[6,64,256]{2,1,0:T(8,128)S(1)} %collective-permute-done.9.refs_9_), channel_id=1, source_target_pairs={{0,1},{1,0},{2,3},{3,2},{4,5},{5,4},{6,7},{7,6},{8,9},{9,8},{10,11... | collective-permute-start | bytes 1179656 | tf_op jit(solution)/shard_map/ppermute | solution.py:21
  33.7 23.5 %collective-permute-start.22 = (f32[6,64,256]{2,1,0:T(8,128)S(1)}, f32[6,64,256]{2,1,0:T(8,128)S(1)}, u32[]{:S(2)}, u32[]{:S(2)}) collective-permute-start(f32[6,64,256]{2,1,0:T(8,128)S(1)} %collective-permute-done.8.refs_8_), channel_id=1, source_target_pairs={{0,8},{4,12},{8,0},{12,4},{16,24},{20,28},{24,16},{28,20},{1,9},{5... | collective-permute-start | bytes 1179656 | tf_op jit(solution)/shard_map/ppermute | solution.py:21
  35.0 22.2 %collective-permute-start.24 = (f32[6,64,256]{2,1,0:T(8,128)S(1)}, f32[6,64,256]{2,1,0:T(8,128)S(1)}, u32[]{:S(2)}, u32[]{:S(2)}) collective-permute-start(f32[6,64,256]{2,1,0:T(8,128)S(1)} %collective-permute-done.23.refs_7_), channel_id=1, source_target_pairs={{0,1},{1,0},{2,3},{3,2},{4,5},{5,4},{6,7},{7,6},{8,9},{9,8},{10,11... | collective-permute-start | bytes 1179656 | tf_op jit(solution)/shard_map/ppermute | solution.py:21
  40.5 11.6 %collective-permute-start.20 = (f32[128,512]{1,0:T(8,128)S(1)}, f32[128,512]{1,0:T(8,128)S(1)}, u32[]{:S(2)}, u32[]{:S(2)}) collective-permute-start(f32[128,512]{1,0:T(8,128)S(1)} %collective-permute-done.19.refs_3_), channel_id=1, source_target_pairs={{0,4},{4,0},{8,12},{12,8},{16,20},{20,16},{24,28},{28,24},{1,5},{5... | collective-permute-start | bytes 786440 | tf_op jit(solution)/shard_map/ppermute | solution.py:21
  40.5 10.6 %collective-permute-start.11 = (f32[64,512]{1,0:T(8,128)S(1)}, f32[64,512]{1,0:T(8,128)S(1)}, u32[]{:S(2)}, u32[]{:S(2)}) collective-permute-start(f32[64,512]{1,0:T(8,128)S(1)} %get-tuple-element.23), channel_id=1, source_target_pairs={{0,8},{4,12},{8,0},{12,4},{16,24},{20,28},{24,16},{28,20},{1,9},{5... | collective-permute-start | bytes 393224 | tf_op jit(solution)/shard_map/ppermute | solution.py:21
  51.1 8.6 %collective-permute-start.13 = (f32[64,512]{1,0:T(8,128)S(1)}, f32[64,512]{1,0:T(8,128)S(1)}, u32[]{:S(2)}, u32[]{:S(2)}) collective-permute-start(f32[64,512]{1,0:T(8,128)S(1)} %add.3.refs_0_), channel_id=1, source_target_pairs={{0,1},{1,0},{2,3},{3,2},{4,5},{5,4},{6,7},{7,6},{8,9},{9,8},{10,11... | collective-permute-start | bytes 393224 | tf_op jit(solution)/shard_map/ppermute | solution.py:21
  52.1 7.7 %collective-permute-start.15 = (f32[64,512]{1,0:T(8,128)S(1)}, f32[64,512]{1,0:T(8,128)S(1)}, u32[]{:S(2)}, u32[]{:S(2)}) collective-permute-start(f32[64,512]{1,0:T(8,128)S(1)} %add.3.refs_0_), channel_id=1, source_target_pairs={{0,2},{1,3},{2,0},{3,1},{4,6},{5,7},{6,4},{7,5},{8,10},{9,11},{10,... | collective-permute-start | bytes 393224 | tf_op jit(solution)/shard_map/ppermute | solution.py:21
  52.6 7.6 %collective-permute-start.17 = (f32[64,512]{1,0:T(8,128)S(1)}, f32[64,512]{1,0:T(8,128)S(1)}, u32[]{:S(2)}, u32[]{:S(2)}) collective-permute-start(f32[64,512]{1,0:T(8,128)S(1)} %add.3.refs_0_), channel_id=1, source_target_pairs={{0,3},{1,2},{2,1},{3,0},{4,7},{5,6},{6,5},{7,4},{8,11},{9,10},{10,... | collective-permute-start | bytes 393224 | tf_op jit(solution)/shard_map/ppermute | solution.py:21
  59.1 13.4 %collective-permute-start.27 = (f32[256,768]{1,0:T(8,128)S(1)}, f32[256,768]{1,0:T(8,128)S(1)}, u32[]{:S(2)}, u32[]{:S(2)}) collective-permute-start(f32[256,768]{1,0:T(8,128)S(1)} %get-tuple-element.31.driven), channel_id=1, source_target_pairs={{0,4},{4,0},{8,12},{12,8},{16,20},{20,16},{24,28},{28,24},{1,5},{5... | collective-permute-start | bytes 2359304 | tf_op jit(solution)/shard_map/ppermute | solution.py:21
  59.2 2.5 %collective-permute-start.12 = (f32[64,512]{1,0:T(8,128)S(1)}, f32[64,512]{1,0:T(8,128)S(1)}, u32[]{:S(2)}, u32[]{:S(2)}) collective-permute-start(f32[64,512]{1,0:T(8,128)S(1)} %add.3.refs_0_), channel_id=1, source_target_pairs={{0,4},{4,0},{8,12},{12,8},{16,20},{20,16},{24,28},{28,24},{1,5},{5... | collective-permute-start | bytes 393224 | tf_op jit(solution)/shard_map/ppermute | solution.py:21
  59.7 2.1 %collective-permute-start.14 = (f32[64,512]{1,0:T(8,128)S(1)}, f32[64,512]{1,0:T(8,128)S(1)}, u32[]{:S(2)}, u32[]{:S(2)}) collective-permute-start(f32[64,512]{1,0:T(8,128)S(1)} %collective-permute-done.13.refs_2_), channel_id=1, source_target_pairs={{0,4},{4,0},{8,12},{12,8},{16,20},{20,16},{24,28},{28,24},{1,5},{5... | collective-permute-start | bytes 393224 | tf_op jit(solution)/shard_map/ppermute | solution.py:21
  59.8 2.3 %collective-permute-start.16 = (f32[64,512]{1,0:T(8,128)S(1)}, f32[64,512]{1,0:T(8,128)S(1)}, u32[]{:S(2)}, u32[]{:S(2)}) collective-permute-start(f32[64,512]{1,0:T(8,128)S(1)} %collective-permute-done.15.refs_4_), channel_id=1, source_target_pairs={{0,4},{4,0},{8,12},{12,8},{16,20},{20,16},{24,28},{28,24},{1,5},{5... | collective-permute-start | bytes 393224 | tf_op jit(solution)/shard_map/ppermute | solution.py:21
  69.7 2.8 %collective-permute-start.26 = (f32[2,64,256]{2,1,0:T(8,128)S(1)}, f32[2,64,256]{2,1,0:T(8,128)S(1)}, u32[]{:S(2)}, u32[]{:S(2)}) collective-permute-start(f32[2,64,256]{2,1,0:T(8,128)S(1)} %copy-done.3), channel_id=1, source_target_pairs={{0,4},{4,0},{8,12},{12,8},{16,20},{20,16},{24,28},{28,24},{1,5},{5... | collective-permute-start | bytes 393224 | tf_op jit(solution)/shard_map/ppermute | solution.py:21
  (9 other events, 16.8 us)

commit v2 on v1

--- a/solution.py
+++ b/solution.py
@@ -65,10 +65,10 @@
     def edge(self, position):
         joint = self.order_two[self.node, position]
         which = joint // 3
-        return which, self.order_one[2 * self.node + which, joint % 3]
+        return which, self.order_one[joint % 3, 2 * self.node + which]
 
     def inner(self, which):
-        return self.order_one[2 * self.node + which, 3]
+        return self.order_one[3, 2 * self.node + which]
 
 
 def block_of(tree, own, other, which, row_edge, start, size, column_edge):
@@ -77,33 +77,40 @@
     return jnp.where(which == tree.half, own[row_edge, rows, column], other[row_edge, rows, column])
 
 
-def first_kernel(order_one, order_two, own, other, data, piece, coupling, bulk):
+def first_kernel(final, order_one, order_two, source, *refs):
+    earlier, (piece, coupling, raw) = refs[:-3], refs[-3:]
+    if final:
+        raw[4:6] = earlier[3][...]
     tree = Tree(order_one, order_two)
     half_width = piece.shape[1]
     width = coupling.shape[1]
+    held = tree.half ^ 1 if final else tree.half
+
+    def keep(out, before, slot, which, row_edge, start, size, column_edge):
+        column = pl.ds(pl.multiple_of(column_edge * W, W), W)
+        value = source[row_edge, pl.ds(start, size), column]
+        other = earlier[before][slot] if final else 0.0
+        out[slot] = jnp.where(which == held, value, other)
+
     start = pl.multiple_of(tree.half * half_width, half_width)
-    total = None
-    for which in range(2):
-        inner = tree.inner(which)
-        part = block_of(tree, own, other, which, inner, start, half_width, inner)
-        total = part if total is None else total + part
-    piece[0] = total
+    inner = tree.inner(held)
+    own_piece = source[inner, pl.ds(start, half_width), pl.ds(pl.multiple_of(inner * W, W), W)]
+    piece[0] = own_piece + earlier[0][0] if final else own_piece
     for slot in range(2):
         which, edge = tree.edge(4 + slot)
-        piece[1 + slot] = block_of(tree, own, other, which, edge, start, half_width, tree.inner(which))
+        keep(piece, 0, 1 + slot, which, edge, start, half_width, tree.inner(which))
     for slot in range(4):
         which, edge = tree.edge(slot)
-        coupling[slot] = block_of(tree, own, other, which, edge, 0, width, tree.inner(which))
+        keep(coupling, 1, slot, which, edge, 0, width, tree.inner(which))
     same, inner_leaf, outer_leaf = packing(tree, tree.node)
     holder = jnp.where(outer_leaf[0] == inner_leaf[0], 0, 1)
     for slot in range(2):
-        bulk[slot] = data[slot]
-        bulk[2 + slot] = coupling[2 * tree.half + slot]
+        raw[slot] = coupling[2 * tree.half + slot]
         row = jnp.where(same, holder, slot)
         column = jnp.where(same, slot, jnp.where(outer_leaf[slot] == inner_leaf[0], 0, 1))
         which, edge = tree.edge(2 * tree.half + row)
         _, column_edge = tree.edge(4 + column)
-        bulk[4 + slot] = block_of(tree, own, other, which, edge, 0, width, column_edge)
+        keep(raw, 2, 2 + slot, which, edge, 0, width, column_edge)
 
 
 def packing(tree, node):
@@ -144,9 +151,12 @@
     start = pl.multiple_of(tree.half * half_width, half_width)
     left = jnp.concatenate([pieces[0][1], pieces[0][2]], axis=0)
     change = product(left, right)
-    for slot in range(2):
-        rows = slice(slot * half_width, (slot + 1) * half_width)
-        inner_rows[rows, :] = interface_rows(tree, own, other, 4 + slot, start, half_width) - change[rows]
+    for slot, (row, column) in enumerate(((0, 0), (0, 1), (1, 1))):
+        which, edge = tree.edge(4 + row)
+        column_which, column_edge = tree.edge(4 + column)
+        value = block_of(tree, own, other, which, edge, start, half_width, column_edge)
+        value = jnp.where(which == column_which, value, 0.0)
+        inner_rows[slot] = value - change[row * half_width : (row + 1) * half_width, column * W : (column + 1) * W]
 
 
 def outer_kernel(order_one, order_two, own, other, coupling, right, outer_all):
@@ -161,29 +171,29 @@
 def third_kernel(count, *refs):
     pieces, (inverse_out, sums) = refs[: 2 * count], refs[2 * count :]
     half, member = lax.axis_index("leaf") % 2, lax.axis_index("sub")
-    half_width = pieces[0].shape[0] // 2
+    half_width = pieces[0].shape[1]
     width = 2 * half_width
     for mask in range(count):
         for side in range(2):
             piece = pieces[2 * mask + side]
-            row = (member ^ mask) * width + (half ^ side) * half_width
-            for slot in range(2):
-                target = pl.ds(pl.multiple_of(row + slot * W, half_width), half_width)
-                sums[target, :] = piece[slot * half_width : (slot + 1) * half_width, :]
+            row = pl.multiple_of((member ^ mask) * width + (half ^ side) * half_width, half_width)
+            sums[pl.ds(row, half_width), :W] = piece[0]
+            sums[pl.ds(row, half_width), W:] = piece[1]
+            sums[pl.ds(pl.multiple_of(row + W, half_width), half_width), W:] = piece[2]
+    sums[W:, :W] = sums[:W, W:].T
     inverse_out[...] = newton(sums[...])
 
 
-def gathered(tree, bulks, data_half, coupling_half, packed_zero, packed_one):
-    width = bulks[0].shape[1]
-    for mask, bulk in enumerate(bulks):
+def gathered(tree, raws, coupling_half, packed_zero, packed_one):
+    for mask, (coupling, packed) in enumerate(raws):
+        width = coupling.shape[1]
         at = (tree.member ^ mask) * width
         for slot in range(2):
             target = pl.ds(pl.multiple_of(slot * W + at, width), width)
-            data_half[target, :] = bulk[slot]
-            coupling_half[target, :] = bulk[2 + slot]
+            coupling_half[target, :] = coupling[slot]
         target = pl.ds(pl.multiple_of(at, width), width)
-        packed_zero[target, :] = bulk[4]
-        packed_one[target, :] = bulk[5]
+        packed_zero[target, :] = packed[0]
+        packed_one[target, :] = packed[1]
 
 
 def outer_rows(tree, node, coupling_split, packed_zero, packed_one, right, outer_half):
@@ -200,11 +210,11 @@
 
 
 def near_kernel(count, order_one, order_two, own, other, coupling, inverse_one, right, *refs):
-    bulks, outs = refs[:count], refs[count:]
-    base_out, outer_half, driven, coupling_half, data_half, packed_zero, packed_one = outs
+    raws, outs = refs[:count], refs[count:]
+    base_out, outer_half, coupling_half, packed_zero, packed_one = outs
     tree = Tree(order_one, order_two)
     width = own.shape[1]
-    gathered(tree, bulks, data_half, coupling_half, packed_zero, packed_one)
+    gathered(tree, [(raw.at[0:2], raw.at[2:4]) for raw in raws], coupling_half, packed_zero, packed_one)
     coupling_split = parts_of(coupling_half[...])
     scaled = product(coupling[...].reshape(4 * width, W), inverse_one[...])
     local = product(scaled, coupling_split, NT)
@@ -217,22 +227,27 @@
             rows, columns = slice(slot * width, (slot + 1) * width), slice(column * W, (column + 1) * W)
             base_out[slot, :, columns] = value - local[rows, columns]
     outer_rows(tree, tree.node, coupling_split, packed_zero, packed_one, right[...], outer_half)
-    turned = parts_of(data_half[...].T)
-    driven[:, : 2 * W] = product(turned, outer_half[...])
-    driven[:, 2 * W :] = product(turned, coupling_split)
-
-
-def far_kernel(count, order_one, order_two, driven_near, right_mine, right_other, *refs):
-    bulks, outs = refs[:count], refs[count:]
-    outer_half, driven, coupling_half, data_half, packed_zero, packed_one, right = outs
-    tree = Tree(order_one, order_two)
-    gathered(tree, bulks, data_half, coupling_half, packed_zero, packed_one)
+
+
+def far_kernel(count, order_one, order_two, outer_near, coupling_near, right_mine, right_other, *refs):
+    raws, last, outs = refs[: 2 * count - 1], refs[2 * count - 1 : 2 * count + 2], refs[2 * count + 2 :]
+    datas = [raw.at[4:6] for raw in raws] + [last[2]]
+    outer_half, driven, coupling_half, packed_zero, packed_one, right, data_half = outs
+    tree = Tree(order_one, order_two)
+    pairs = [(raw.at[0:2], raw.at[2:4]) for raw in raws[count:]] + [last[:2]]
+    gathered(tree, pairs, coupling_half, packed_zero, packed_one)
     for side, held in enumerate((right_mine, right_other)):
         right[pl.ds(pl.multiple_of((tree.half ^ side) * (W // 2), W // 2), W // 2), :] = held[...]
-    node = tree.node ^ 1
-    outer_rows(tree, node, parts_of(coupling_half[...]), packed_zero, packed_one, right[...], outer_half)
-    driven[:, : 2 * W] = driven_near[:, : 2 * W] + product(data_half[...].T, outer_half[...])
-    driven[:, 2 * W :] = driven_near[:, 2 * W :]
+    outer_rows(tree, tree.node ^ 1, parts_of(coupling_half[...]), packed_zero, packed_one, right[...], outer_half)
+    for place, data in enumerate(datas):
+        width = data.shape[1]
+        at = (tree.member ^ (place % count)) * width + (place // count) * 2 * W
+        for slot in range(2):
+            data_half[pl.ds(pl.multiple_of(slot * W + at, width), width), :] = data[slot]
+    near = parts_of(data_half[: 2 * W, :].T)
+    far = data_half[2 * W :, :].T
+    driven[:, : 2 * W] = product(near, outer_near[...]) + product(far, outer_half[...])
+    driven[:, 2 * W :] = product(near, coupling_near[...])
 
 
 def top_kernel(base, outer_all, inverse_two, outer_near, outer_far, mine, theirs):
@@ -258,7 +273,7 @@
     mine = pl.multiple_of(tree.member * width, width)
     rows = [inverse_two[pl.ds(pl.multiple_of(slot * W + mine, width), width), :] for slot in range(2)]
     inner[...] = -product(jnp.concatenate(rows, axis=0), second, NT)
-    leaf_data[tree.order_one[tree.leaf, 3]] = -product(inverse_one[pl.ds(mine, width), :], first, NT)
+    leaf_data[order_one[3, tree.leaf]] = -product(inverse_one[pl.ds(mine, width), :], first, NT)
     for slot in range(3):
         joint = 3 * tree.half + slot
         position = 0
@@ -267,7 +282,7 @@
         place = position % 2
         from_data = jnp.where(position // 2 == tree.half, data_own[place], data_other[place])
         from_inner = inner[pl.ds(pl.multiple_of(place * width, width), width), :]
-        leaf_data[order_one[tree.leaf, slot]] = jnp.where(position < 4, from_data, from_inner)
+        leaf_data[order_one[slot, tree.leaf]] = jnp.where(position < 4, from_data, from_inner)
 
 
 def join_kernel(mine, theirs, top_map):
@@ -298,7 +313,7 @@
     half_width = width // 2
     count = lax.axis_size("sub")
     bits = [("sub", 2**bit) for bit in range((count - 1).bit_length())] + [("leaf", 2)]
-    orders = (order_one, order_two)
+    orders = (order_one.T, order_two)
 
     def across(value):
         found = {0: value}
@@ -306,47 +321,57 @@
             found[mask] = swapped(value, "sub", mask)
         return [found[mask] for mask in range(count)]
 
-    def spread(value, used):
+    def spread(value, last):
         found = {0: value}
-        for mask in sorted(range(1, 2 ** len(used)), key=lambda m: (bin(m).count("1"), m)):
-            held = [bit for bit in range(len(used)) if mask >> bit & 1]
-            chosen = next((bit for bit in held if (bit + 1) % len(used) in held), held[0])
-            found[mask] = swapped(found[mask ^ (1 << chosen)], *used[chosen])
-        return [found[mask] for mask in range(2 ** len(used))]
+        for mask in sorted(range(1, 2 * count - 1), key=lambda m: (bin(m).count("1"), m)):
+            held = [bit for bit in range(len(bits)) if mask >> bit & 1]
+            chosen = next((bit for bit in held if (bit + 1) % len(bits) in held), held[0])
+            found[mask] = swapped(found[mask ^ (1 << chosen)], *bits[chosen])
+        top = 2 * count - 1
+        found[top] = []
+        for first, end, chosen in last:
+            found[top].append(swapped(found[top ^ (1 << chosen)][first:end], *bits[chosen]))
+        return [found[mask] for mask in range(2 * count)]
 
     def with_sibling(values):
-        return [item for value in values for item in (value, swapped(value, "leaf", 1))]
+        found = []
+        for value in values:
+            found += [value, swapped(value, "leaf", 1)]
+        return found
 
     other = swapped(leaf_maps, "leaf", 1)
-    piece, coupling, bulk = call(
-        first_kernel, 2, [(3, half_width, W), (4, width, W), (6, width, W)], [],
-        *orders, leaf_maps, other, top_data,
-    )
+    first_outs = [(3, half_width, W), (4, width, W)]
+    early = call(lambda *refs: first_kernel(False, *refs), 2, first_outs + [(4, width, W)], [], *orders, leaf_maps)
+    piece, coupling, raw = call(
+        lambda *refs: first_kernel(True, *refs), 2, first_outs + [(6, width, W)], [], *orders, other, *early, top_data
+    )
+    own = leaf_maps
     pieces = with_sibling(across(piece))
     data_other = swapped(top_data, "leaf", 1)
-    bulks = spread(bulk, bits)
+    raws = spread(raw, [(2 * part, 2 * part + 2, part % len(bits)) for part in range(3)])
     inner_rows, inverse_one, coupling_inner, right, right_half = call(
         lambda *refs: second_kernel(count, *refs), 2,
-        [(2 * half_width, 2 * W), (W, W), (2 * W, W), (W, 2 * W), (W // 2, 2 * W)], [(W, W)],
-        *orders, leaf_maps, other, *pieces,
+        [(3, half_width, W), (W, W), (2 * W, W), (W, 2 * W), (W // 2, 2 * W)], [(W, W)],
+        *orders, own, other, *pieces,
     )
     summed = inner_rows + swapped(inner_rows, "leaf", 2)
     right_mine = swapped(right_half, "leaf", 2)
     right_other = swapped(right_mine, "leaf", 1)
-    (outer_all,) = call(outer_kernel, 2, [(4, width, 2 * W)], [], *orders, leaf_maps, other, coupling, right)
+    (outer_all,) = call(outer_kernel, 2, [(4, width, 2 * W)], [], *orders, own, other, coupling, right)
     (inverse_two,) = call(
         lambda *refs: third_kernel(count, *refs), 0, [(2 * W, 2 * W)], [(2 * W, 2 * W)],
         *with_sibling(across(summed)),
     )
-    scratch = [(2 * W, W), (2 * W, K), (W, W), (W, W)]
-    base, outer_near, driven_near = call(
+    base, outer_near, coupling_near = call(
         lambda *refs: near_kernel(count, *refs), 2,
-        [(4, width, 2 * W), (2 * W, 2 * W), (K, 3 * W)], scratch,
-        *orders, leaf_maps, other, coupling, inverse_one, right, *bulks[:count],
+        [(4, width, 2 * W), (2 * W, 2 * W), (2 * W, W)], [(W, W), (W, W)],
+        *orders, own, other, coupling, inverse_one, right, *raws[:count],
     )
     outer_far, driven = call(
-        lambda *refs: far_kernel(count, *refs), 2, [(2 * W, 2 * W), (K, 3 * W)], scratch + [(W, 2 * W)],
-        *orders, driven_near, right_mine, right_other, *bulks[count:],
+        lambda *refs: far_kernel(count, *refs), 2, [(2 * W, 2 * W), (K, 3 * W)],
+        [(2 * W, W), (W, W), (W, W), (W, 2 * W), (4 * W, K)],
+        *orders, outer_near, coupling_near, right_mine, right_other,
+        *raws[:-1], *raws[-1],
     )
     driven_other = swapped(driven, "leaf", 1)
     mine, theirs = call(top_kernel, 0, [(2, width, 4 * W)] * 2, [], base, outer_all, inverse_two, outer_near, outer_far)

time: 75.5 us -> 83.8 us (1.11)
  waiting for transfers between devices: 30.7 us -> 35.1 us
  starting transfers between devices: 20.9 us -> 24.2 us
    ppermute x28 -> x30, waiting for transfers between devices: 30.7 us -> 35.1 us  [swapped(): return lax.ppermute(value, axis, pairs)]
    ppermute x28 -> x30, starting transfers between devices: 20.9 us -> 24.2 us  [swapped(): return lax.ppermute(value, axis, pairs)]
    pallas_call x9 -> x10, Pallas kernels: 20.1 us -> 20.7 us  [call(): pl.pallas_call(kernel, in_specs=[smem] * scalar_count + [vmem] * (len(arg...]
    unnamed x11 -> x14, local copies, waits for them, and re-layouts: 2.9 us -> 2.68 us
  transfers between devices with their start and end apart: 28 -> 30, of which waited for: 13 -> 12; matrix products, arithmetic and copies ran while one was open for 1% -> 0% of each run, Pallas kernels for 22% -> 21%
where the time goes in v2:
time: 83.8 us; the launch traced here: 83.6 us
  waiting for transfers between devices  35.1 us (42%)
  starting transfers between devices  24.2 us (29%)
  Pallas kernels  20.7 us (25%)
  local copies, waits for them, and re-layouts  2.7 us (3%)
    ppermute x30, waiting for transfers between devices, swapped(): return lax.ppermute(value, axis, pairs)  35.1 us
    ppermute x30, starting transfers between devices, swapped(): return lax.ppermute(value, axis, pairs)  24.2 us
    pallas_call x10, Pallas kernels, call(): pl.pallas_call(kernel, in_specs=[smem] * scalar_count + [vmem] * (len(arg...  20.7 us
    unnamed x14, local copies, waits for them, and re-layouts  2.68 us
  transfers between devices with their start and end apart: 30, of which 12 were waited for; matrix products, arithmetic and copies ran while one was open for 0% of the time, Pallas kernels for 21%

profile of v2, /device:TPU:0, one launch (start us, length us, event | category | flops | bytes accessed | tf_op | source)
XLA Modules:
  0.0 83.6 jit_solution(5750116117706305880)
XLA Ops:
  5.5 3.1 %collective-permute-start.21 = (f32[6,64,256]{2,1,0:T(8,128)S(1)}, f32[6,64,256]{2,1,0:T(8,128)S(1)}, u32[]{:S(2)}, u32[]{:S(2)}) collective-permute-start(f32[6,64,256]{2,1,0:T(8,128)S(1)} %get-tuple-element.27.refs_7_.refs_6_), channel_id=1, source_target_pairs={{0,8},{4,12},{8,0},{12,4},{16,24},{20,28},{24,16},{28,20},{1,9},{5... | collective-permute-start | bytes 1179656 | tf_op jit(solution)/shard_map/ppermute | solution.py:21
  8.6 1.5 %collective-permute-start.8 = (f32[6,64,256]{2,1,0:T(8,128)S(1)}, f32[6,64,256]{2,1,0:T(8,128)S(1)}, u32[]{:S(2)}, u32[]{:S(2)}) collective-permute-start(f32[6,64,256]{2,1,0:T(8,128)S(1)} %get-tuple-element.27.refs_7_.refs_6_), channel_id=1, source_target_pairs={{0,1},{1,0},{2,3},{3,2},{4,5},{5,4},{6,7},{7,6},{8,9},{9,8},{10,11... | collective-permute-start | bytes 1179656 | tf_op jit(solution)/shard_map/ppermute | solution.py:21
  10.1 1.5 %collective-permute-start.9 = (f32[6,64,256]{2,1,0:T(8,128)S(1)}, f32[6,64,256]{2,1,0:T(8,128)S(1)}, u32[]{:S(2)}, u32[]{:S(2)}) collective-permute-start(f32[6,64,256]{2,1,0:T(8,128)S(1)} %get-tuple-element.27.refs_7_.refs_6_), channel_id=1, source_target_pairs={{0,2},{1,3},{2,0},{3,1},{4,6},{5,7},{6,4},{7,5},{8,10},{9,11},{10,... | collective-permute-start | bytes 1179656 | tf_op jit(solution)/shard_map/ppermute | solution.py:21
  12.7 8.9 %collective-permute-done.2.refs_6_ = f32[3,32,256]{2,1,0:T(8,128)S(1)} collective-permute-done((f32[3,32,256]{2,1,0:T(8,128)S(1)}, f32[3,32,256]{2,1,0:T(8,128)S(1)}, u32[]{:S(2)}, u32[]{:S(2)}) %collective-permute-start.2) | collective-permute-done | bytes 98336 | tf_op jit(solution)/shard_map/ppermute | solution.py:21
  21.5 2.4 %collective-permute-start.6 = (f32[3,32,256]{2,1,0:T(8,128)S(1)}, f32[3,32,256]{2,1,0:T(8,128)S(1)}, u32[]{:S(2)}, u32[]{:S(2)}) collective-permute-start(f32[3,32,256]{2,1,0:T(8,128)S(1)} %get-tuple-element.24.refs_4_), channel_id=1, source_target_pairs={{0,3},{1,2},{2,1},{3,0},{4,7},{5,6},{6,5},{7,4},{8,11},{9,10},{10,... | collective-permute-start | bytes 294920 | tf_op jit(solution)/shard_map/ppermute | solution.py:21
  24.0 3.1 %collective-permute-done.6.refs_10_ = f32[3,32,256]{2,1,0:T(8,128)S(1)} collective-permute-done((f32[3,32,256]{2,1,0:T(8,128)S(1)}, f32[3,32,256]{2,1,0:T(8,128)S(1)}, u32[]{:S(2)}, u32[]{:S(2)}) %collective-permute-start.6) | collective-permute-done | bytes 98336 | tf_op jit(solution)/shard_map/ppermute | solution.py:21
  28.5 2.7 %shard_map.61 = (f32[3,32,256]{2,1,0:T(8,128)S(1)}, f32[256,256]{1,0:T(8,128)S(1)}, f32[512,256]{1,0:T(8,128)S(1)}, f32[256,512]{1,0:T(8,128)S(1)}, f32[128,512]{1,0:T(8,128)S(1)}) custom-call(s32[4,8]{1,0:T(4,128)S(1)} %bitcast.3, s32[4,6]{1,0:T(4,128)S(1)} %copy-done.5, f32[4,64,1024]{2,1,0:T(8,128)S(1)} %copy-done.1, ...), custom_call_target="tpu_custom_call" | custom-call | tf_op jit(solution)/shard_map/pallas_call | solution.py:301
  31.2 1.6 %collective-permute-start.23 = (f32[6,64,256]{2,1,0:T(8,128)S(1)}, f32[6,64,256]{2,1,0:T(8,128)S(1)}, u32[]{:S(2)}, u32[]{:S(2)}) collective-permute-start(f32[6,64,256]{2,1,0:T(8,128)S(1)} %collective-permute-done.21.refs_10_), channel_id=1, source_target_pairs={{0,2},{1,3},{2,0},{3,1},{4,6},{5,7},{6,4},{7,5},{8,10},{9,11},{10,... | collective-permute-start | bytes 1179656 | tf_op jit(solution)/shard_map/ppermute | solution.py:21
  33.3 1.6 %collective-permute-start.19 = (f32[128,512]{1,0:T(8,128)S(1)}, f32[128,512]{1,0:T(8,128)S(1)}, u32[]{:S(2)}, u32[]{:S(2)}) collective-permute-start(f32[128,512]{1,0:T(8,128)S(1)} %get-tuple-element.32), channel_id=1, source_target_pairs={{0,8},{4,12},{8,0},{12,4},{16,24},{20,28},{24,16},{28,20},{1,9},{5... | collective-permute-start | bytes 786440 | tf_op jit(solution)/shard_map/ppermute | solution.py:21
  34.9 1.5 %collective-permute-start.10 = (f32[6,64,256]{2,1,0:T(8,128)S(1)}, f32[6,64,256]{2,1,0:T(8,128)S(1)}, u32[]{:S(2)}, u32[]{:S(2)}) collective-permute-start(f32[6,64,256]{2,1,0:T(8,128)S(1)} %collective-permute-done.9.refs_9_.refs_8_), channel_id=1, source_target_pairs={{0,1},{1,0},{2,3},{3,2},{4,5},{5,4},{6,7},{7,6},{8,9},{9,8},{10,11... | collective-permute-start | bytes 1179656 | tf_op jit(solution)/shard_map/ppermute | solution.py:21
  36.3 13.2 %collective-permute-done.19.refs_4_ = f32[128,512]{1,0:T(8,128)S(1)} collective-permute-done((f32[128,512]{1,0:T(8,128)S(1)}, f32[128,512]{1,0:T(8,128)S(1)}, u32[]{:S(2)}, u32[]{:S(2)}) %collective-permute-start.19) | collective-permute-done | bytes 262176 | tf_op jit(solution)/shard_map/ppermute | solution.py:21
  49.6 1.6 %collective-permute-start.24 = (f32[2,64,256]{2,1,0:T(8,128)S(1)}, f32[2,64,256]{2,1,0:T(8,128)S(1)}, u32[]{:S(2)}, u32[]{:S(2)}) collective-permute-start(f32[2,64,256]{2,1,0:T(8,128)S(1)} %slice.12), channel_id=1, source_target_pairs={{0,1},{1,0},{2,3},{3,2},{4,5},{5,4},{6,7},{7,6},{8,9},{9,8},{10,11... | collective-permute-start | bytes 393224 | tf_op jit(solution)/shard_map/ppermute | solution.py:21
  52.2 1.6 %collective-permute-start.11 = (f32[3,32,256]{2,1,0:T(8,128)S(1)}, f32[3,32,256]{2,1,0:T(8,128)S(1)}, u32[]{:S(2)}, u32[]{:S(2)}) collective-permute-start(f32[3,32,256]{2,1,0:T(8,128)S(1)} %get-tuple-element.29), channel_id=1, source_target_pairs={{0,8},{4,12},{8,0},{12,4},{16,24},{20,28},{24,16},{28,20},{1,9},{5... | collective-permute-start | bytes 294920 | tf_op jit(solution)/shard_map/ppermute | solution.py:21
  53.8 1.8 %shard_map.62 = (f32[4,64,512]{2,1,0:T(8,128)S(1)}, f32[512,512]{1,0:T(8,128)S(1)}, f32[512,256]{1,0:T(8,128)S(1)}) custom-call(s32[4,8]{1,0:T(4,128)S(1)} %bitcast.4, s32[4,6]{1,0:T(4,128)S(1)} %copy-done.5, f32[4,64,1024]{2,1,0:T(8,128)S(1)} %copy-done.1, f32[4,64,1024]{2,1,0:T(8,128)S(1)} %collective-permute-done.refs_2_.refs_3_.other, ...), custom_call_target="tpu_custom_call" | custom-call | tf_op jit(solution)/shard_map/pallas_call | solution.py:301
  56.8 1.3 %collective-permute-done.26.refs_15_ = f32[2,64,256]{2,1,0:T(8,128)S(1)} collective-permute-done((f32[2,64,256]{2,1,0:T(8,128)S(1)}, f32[2,64,256]{2,1,0:T(8,128)S(1)}, u32[]{:S(2)}, u32[]{:S(2)}) %collective-permute-start.26) | collective-permute-done | bytes 131104 | tf_op jit(solution)/shard_map/ppermute | solution.py:21
  58.2 2.5 %shard_map.65 = (f32[512,512]{1,0:T(8,128)S(1)}, f32[256,768]{1,0:T(8,128)S(1)}) custom-call(s32[4,8]{1,0:T(4,128)S(1)} %bitcast.5, s32[4,6]{1,0:T(4,128)S(1)} %copy-done.5, f32[512,512]{1,0:T(8,128)S(1)} %get-tuple-element.30.refs_2_.outer_near, f32[512,256]{1,0:T(8,128)S(1)} %get-tuple-element.31.refs_3_, f32[128,512]{1,0:T(8,128)S(1)} %collective-permute-done.19.refs_4_, ...), custom_call_target="tpu_custom_call" | custom-call | tf_op jit(solution)/shard_map/pallas_call | solution.py:301
  61.4 1.5 %collective-permute-start.15 = (f32[3,32,256]{2,1,0:T(8,128)S(1)}, f32[3,32,256]{2,1,0:T(8,128)S(1)}, u32[]{:S(2)}, u32[]{:S(2)}) collective-permute-start(f32[3,32,256]{2,1,0:T(8,128)S(1)} %add.3.refs_0_), channel_id=1, source_target_pairs={{0,2},{1,3},{2,0},{3,1},{4,6},{5,7},{6,4},{7,5},{8,10},{9,11},{10,... | collective-permute-start | bytes 294920 | tf_op jit(solution)/shard_map/ppermute | solution.py:21
  63.0 1.4 %collective-permute-start.17 = (f32[3,32,256]{2,1,0:T(8,128)S(1)}, f32[3,32,256]{2,1,0:T(8,128)S(1)}, u32[]{:S(2)}, u32[]{:S(2)}) collective-permute-start(f32[3,32,256]{2,1,0:T(8,128)S(1)} %add.3.refs_0_), channel_id=1, source_target_pairs={{0,3},{1,2},{2,1},{3,0},{4,7},{5,6},{6,5},{7,4},{8,11},{9,10},{10,... | collective-permute-start | bytes 294920 | tf_op jit(solution)/shard_map/ppermute | solution.py:21
  64.4 2.2 %collective-permute-done.13.refs_2_ = f32[3,32,256]{2,1,0:T(8,128)S(1)} collective-permute-done((f32[3,32,256]{2,1,0:T(8,128)S(1)}, f32[3,32,256]{2,1,0:T(8,128)S(1)}, u32[]{:S(2)}, u32[]{:S(2)}) %collective-permute-start.13) | collective-permute-done | bytes 98336 | tf_op jit(solution)/shard_map/ppermute | solution.py:21
  67.5 1.6 %collective-permute-done.17.refs_6_ = f32[3,32,256]{2,1,0:T(8,128)S(1)} collective-permute-done((f32[3,32,256]{2,1,0:T(8,128)S(1)}, f32[3,32,256]{2,1,0:T(8,128)S(1)}, u32[]{:S(2)}, u32[]{:S(2)}) %collective-permute-start.17) | collective-permute-done | bytes 98336 | tf_op jit(solution)/shard_map/ppermute | solution.py:21
  70.4 5.7 %shard_map.64.inverse_two = f32[512,512]{1,0:T(8,128)S(1)} custom-call(f32[3,32,256]{2,1,0:T(8,128)S(1)} %add.3.refs_0_, f32[3,32,256]{2,1,0:T(8,128)S(1)} %collective-permute-done.12.refs_1_, f32[3,32,256]{2,1,0:T(8,128)S(1)} %collective-permute-done.13.refs_2_, f32[3,32,256]{2,1,0:T(8,128)S(1)} %collective-permute-done.14.refs_3_, ...), custom_call_target="tpu_custom_call" | custom-call | tf_op jit(solution)/shard_map/pallas_call | solution.py:301
  76.2 1.6 %shard_map.66 = (f32[2,64,1024]{2,1,0:T(8,128)S(1)}, f32[2,64,1024]{2,1,0:T(8,128)S(1)}) custom-call(f32[4,64,512]{2,1,0:T(8,128)S(1)} %get-tuple-element.28.base, f32[4,64,512]{2,1,0:T(8,128)S(1)} %shard_map.63.outer_all, f32[512,512]{1,0:T(8,128)S(1)} %shard_map.64.inverse_two, f32[512,512]{1,0:T(8,128)S(1)} %get-tuple-element.30.refs_2_.outer_near, ...), custom_call_target="tpu_custom_call" | custom-call | tf_op jit(solution)/shard_map/pallas_call | solution.py:301
  78.4 1.4 %collective-permute-done.27.theirs = f32[2,64,1024]{2,1,0:T(8,128)S(1)} collective-permute-done((f32[2,64,1024]{2,1,0:T(8,128)S(1)}, f32[2,64,1024]{2,1,0:T(8,128)S(1)}, u32[]{:S(2)}, u32[]{:S(2)}) %collective-permute-start.27) | collective-permute-done | bytes 524320 | tf_op jit(solution)/shard_map/ppermute | solution.py:21
  80.9 2.7 %shard_map.68 = f32[4,64,256]{2,1,0:T(8,128)} custom-call(s32[4,8]{1,0:T(4,128)S(1)} %bitcast.7, s32[4,6]{1,0:T(4,128)S(1)} %copy-done.6, f32[2,64,256]{2,1,0:T(8,128)S(1)} %copy-done.2, f32[2,64,256]{2,1,0:T(8,128)S(1)} %collective-permute-done.28.data_other, f32[512,256]{1,0:T(8,128)S(1)} %get-tuple-element.36.coupling_inner, ...), custom_call_target="tpu_custom_call" | custom-call | tf_op jit(solution)/shard_map/pallas_call | solution.py:301
  (64 shorter events, 14.7 us)
Async XLA Ops:
  0.6 4.0 %collective-permute-start = (f32[4,64,1024]{2,1,0:T(8,128)}, f32[4,64,1024]{2,1,0:T(8,128)S(1)}, u32[]{:S(2)}, u32[]{:S(2)}) collective-permute-start(f32[4,64,1024]{2,1,0:T(8,128)} %own.1), channel_id=1, source_target_pairs={{0,4},{4,0},{8,12},{12,8},{16,20},{20,16},{24,28},{28,24},{1,5},{5... | collective-permute-start | bytes 3145736 | tf_op jit(solution)/shard_map/ppermute | solution.py:21
  5.5 6.7 %collective-permute-start.1 = (f32[3,32,256]{2,1,0:T(8,128)S(1)}, f32[3,32,256]{2,1,0:T(8,128)S(1)}, u32[]{:S(2)}, u32[]{:S(2)}) collective-permute-start(f32[3,32,256]{2,1,0:T(8,128)S(1)} %get-tuple-element.24.refs_4_), channel_id=1, source_target_pairs={{0,4},{4,0},{8,12},{12,8},{16,20},{20,16},{24,28},{28,24},{1,5},{5... | collective-permute-start | bytes 294920 | tf_op jit(solution)/shard_map/ppermute | solution.py:21
  5.5 25.7 %collective-permute-start.21 = (f32[6,64,256]{2,1,0:T(8,128)S(1)}, f32[6,64,256]{2,1,0:T(8,128)S(1)}, u32[]{:S(2)}, u32[]{:S(2)}) collective-permute-start(f32[6,64,256]{2,1,0:T(8,128)S(1)} %get-tuple-element.27.refs_7_.refs_6_), channel_id=1, source_target_pairs={{0,8},{4,12},{8,0},{12,4},{16,24},{20,28},{24,16},{28,20},{1,9},{5... | collective-permute-start | bytes 1179656 | tf_op jit(solution)/shard_map/ppermute | solution.py:21
  8.6 24.2 %collective-permute-start.8 = (f32[6,64,256]{2,1,0:T(8,128)S(1)}, f32[6,64,256]{2,1,0:T(8,128)S(1)}, u32[]{:S(2)}, u32[]{:S(2)}) collective-permute-start(f32[6,64,256]{2,1,0:T(8,128)S(1)} %get-tuple-element.27.refs_7_.refs_6_), channel_id=1, source_target_pairs={{0,1},{1,0},{2,3},{3,2},{4,5},{5,4},{6,7},{7,6},{8,9},{9,8},{10,11... | collective-permute-start | bytes 1179656 | tf_op jit(solution)/shard_map/ppermute | solution.py:21
  10.1 24.8 %collective-permute-start.9 = (f32[6,64,256]{2,1,0:T(8,128)S(1)}, f32[6,64,256]{2,1,0:T(8,128)S(1)}, u32[]{:S(2)}, u32[]{:S(2)}) collective-permute-start(f32[6,64,256]{2,1,0:T(8,128)S(1)} %get-tuple-element.27.refs_7_.refs_6_), channel_id=1, source_target_pairs={{0,2},{1,3},{2,0},{3,1},{4,6},{5,7},{6,4},{7,5},{8,10},{9,11},{10,... | collective-permute-start | bytes 1179656 | tf_op jit(solution)/shard_map/ppermute | solution.py:21
  11.6 9.9 %collective-permute-start.2 = (f32[3,32,256]{2,1,0:T(8,128)S(1)}, f32[3,32,256]{2,1,0:T(8,128)S(1)}, u32[]{:S(2)}, u32[]{:S(2)}) collective-permute-start(f32[3,32,256]{2,1,0:T(8,128)S(1)} %get-tuple-element.24.refs_4_), channel_id=1, source_target_pairs={{0,1},{1,0},{2,3},{3,2},{4,5},{5,4},{6,7},{7,6},{8,9},{9,8},{10,11... | collective-permute-start | bytes 294920 | tf_op jit(solution)/shard_map/ppermute | solution.py:21
  12.1 11.8 %collective-permute-start.4 = (f32[3,32,256]{2,1,0:T(8,128)S(1)}, f32[3,32,256]{2,1,0:T(8,128)S(1)}, u32[]{:S(2)}, u32[]{:S(2)}) collective-permute-start(f32[3,32,256]{2,1,0:T(8,128)S(1)} %get-tuple-element.24.refs_4_), channel_id=1, source_target_pairs={{0,2},{1,3},{2,0},{3,1},{4,6},{5,7},{6,4},{7,5},{8,10},{9,11},{10,... | collective-permute-start | bytes 294920 | tf_op jit(solution)/shard_map/ppermute | solution.py:21
  21.5 5.5 %collective-permute-start.6 = (f32[3,32,256]{2,1,0:T(8,128)S(1)}, f32[3,32,256]{2,1,0:T(8,128)S(1)}, u32[]{:S(2)}, u32[]{:S(2)}) collective-permute-start(f32[3,32,256]{2,1,0:T(8,128)S(1)} %get-tuple-element.24.refs_4_), channel_id=1, source_target_pairs={{0,3},{1,2},{2,1},{3,0},{4,7},{5,6},{6,5},{7,4},{8,11},{9,10},{10,... | collective-permute-start | bytes 294920 | tf_op jit(solution)/shard_map/ppermute | solution.py:21
  24.0 3.1 %collective-permute-start.3 = (f32[3,32,256]{2,1,0:T(8,128)S(1)}, f32[3,32,256]{2,1,0:T(8,128)S(1)}, u32[]{:S(2)}, u32[]{:S(2)}) collective-permute-start(f32[3,32,256]{2,1,0:T(8,128)S(1)} %collective-permute-done.2.refs_6_), channel_id=1, source_target_pairs={{0,4},{4,0},{8,12},{12,8},{16,20},{20,16},{24,28},{28,24},{1,5},{5... | collective-permute-start | bytes 294920 | tf_op jit(solution)/shard_map/ppermute | solution.py:21
  31.2 18.3 %collective-permute-start.23 = (f32[6,64,256]{2,1,0:T(8,128)S(1)}, f32[6,64,256]{2,1,0:T(8,128)S(1)}, u32[]{:S(2)}, u32[]{:S(2)}) collective-permute-start(f32[6,64,256]{2,1,0:T(8,128)S(1)} %collective-permute-done.21.refs_10_), channel_id=1, source_target_pairs={{0,2},{1,3},{2,0},{3,1},{4,6},{5,7},{6,4},{7,5},{8,10},{9,11},{10,... | collective-permute-start | bytes 1179656 | tf_op jit(solution)/shard_map/ppermute | solution.py:21
  32.8 18.3 %collective-permute-start.22 = (f32[6,64,256]{2,1,0:T(8,128)S(1)}, f32[6,64,256]{2,1,0:T(8,128)S(1)}, u32[]{:S(2)}, u32[]{:S(2)}) collective-permute-start(f32[6,64,256]{2,1,0:T(8,128)S(1)} %collective-permute-done.8.refs_8_.refs_7_), channel_id=1, source_target_pairs={{0,8},{4,12},{8,0},{12,4},{16,24},{20,28},{24,16},{28,20},{1,9},{5... | collective-permute-start | bytes 1179656 | tf_op jit(solution)/shard_map/ppermute | solution.py:21
  33.3 16.3 %collective-permute-start.19 = (f32[128,512]{1,0:T(8,128)S(1)}, f32[128,512]{1,0:T(8,128)S(1)}, u32[]{:S(2)}, u32[]{:S(2)}) collective-permute-start(f32[128,512]{1,0:T(8,128)S(1)} %get-tuple-element.32), channel_id=1, source_target_pairs={{0,8},{4,12},{8,0},{12,4},{16,24},{20,28},{24,16},{28,20},{1,9},{5... | collective-permute-start | bytes 786440 | tf_op jit(solution)/shard_map/ppermute | solution.py:21
  34.9 16.9 %collective-permute-start.10 = (f32[6,64,256]{2,1,0:T(8,128)S(1)}, f32[6,64,256]{2,1,0:T(8,128)S(1)}, u32[]{:S(2)}, u32[]{:S(2)}) collective-permute-start(f32[6,64,256]{2,1,0:T(8,128)S(1)} %collective-permute-done.9.refs_9_.refs_8_), channel_id=1, source_target_pairs={{0,1},{1,0},{2,3},{3,2},{4,5},{5,4},{6,7},{7,6},{8,9},{9,8},{10,11... | collective-permute-start | bytes 1179656 | tf_op jit(solution)/shard_map/ppermute | solution.py:21
  49.5 6.0 %collective-permute-start.20 = (f32[128,512]{1,0:T(8,128)S(1)}, f32[128,512]{1,0:T(8,128)S(1)}, u32[]{:S(2)}, u32[]{:S(2)}) collective-permute-start(f32[128,512]{1,0:T(8,128)S(1)} %collective-permute-done.19.refs_4_), channel_id=1, source_target_pairs={{0,4},{4,0},{8,12},{12,8},{16,20},{20,16},{24,28},{28,24},{1,5},{5... | collective-permute-start | bytes 786440 | tf_op jit(solution)/shard_map/ppermute | solution.py:21
  49.6 6.0 %collective-permute-start.24 = (f32[2,64,256]{2,1,0:T(8,128)S(1)}, f32[2,64,256]{2,1,0:T(8,128)S(1)}, u32[]{:S(2)}, u32[]{:S(2)}) collective-permute-start(f32[2,64,256]{2,1,0:T(8,128)S(1)} %slice.12), channel_id=1, source_target_pairs={{0,1},{1,0},{2,3},{3,2},{4,5},{5,4},{6,7},{7,6},{8,9},{9,8},{10,11... | collective-permute-start | bytes 393224 | tf_op jit(solution)/shard_map/ppermute | solution.py:21
  51.1 5.7 %collective-permute-start.25 = (f32[2,64,256]{2,1,0:T(8,128)S(1)}, f32[2,64,256]{2,1,0:T(8,128)S(1)}, u32[]{:S(2)}, u32[]{:S(2)}) collective-permute-start(f32[2,64,256]{2,1,0:T(8,128)S(1)} %slice.13), channel_id=1, source_target_pairs={{0,2},{1,3},{2,0},{3,1},{4,6},{5,7},{6,4},{7,5},{8,10},{9,11},{10,... | collective-permute-start | bytes 393224 | tf_op jit(solution)/shard_map/ppermute | solution.py:21
  51.7 6.4 %collective-permute-start.26 = (f32[2,64,256]{2,1,0:T(8,128)S(1)}, f32[2,64,256]{2,1,0:T(8,128)S(1)}, u32[]{:S(2)}, u32[]{:S(2)}) collective-permute-start(f32[2,64,256]{2,1,0:T(8,128)S(1)} %slice.14), channel_id=1, source_target_pairs={{0,8},{4,12},{8,0},{12,4},{16,24},{20,28},{24,16},{28,20},{1,9},{5... | collective-permute-start | bytes 393224 | tf_op jit(solution)/shard_map/ppermute | solution.py:21
  52.2 8.6 %collective-permute-start.11 = (f32[3,32,256]{2,1,0:T(8,128)S(1)}, f32[3,32,256]{2,1,0:T(8,128)S(1)}, u32[]{:S(2)}, u32[]{:S(2)}) collective-permute-start(f32[3,32,256]{2,1,0:T(8,128)S(1)} %get-tuple-element.29), channel_id=1, source_target_pairs={{0,8},{4,12},{8,0},{12,4},{16,24},{20,28},{24,16},{28,20},{1,9},{5... | collective-permute-start | bytes 294920 | tf_op jit(solution)/shard_map/ppermute | solution.py:21
  60.7 20.1 %collective-permute-start.29 = (f32[256,768]{1,0:T(8,128)S(1)}, f32[256,768]{1,0:T(8,128)S(1)}, u32[]{:S(2)}, u32[]{:S(2)}) collective-permute-start(f32[256,768]{1,0:T(8,128)S(1)} %get-tuple-element.37.driven), channel_id=1, source_target_pairs={{0,4},{4,0},{8,12},{12,8},{16,20},{20,16},{24,28},{28,24},{1,5},{5... | collective-permute-start | bytes 2359304 | tf_op jit(solution)/shard_map/ppermute | solution.py:21
  60.8 5.7 %collective-permute-start.13 = (f32[3,32,256]{2,1,0:T(8,128)S(1)}, f32[3,32,256]{2,1,0:T(8,128)S(1)}, u32[]{:S(2)}, u32[]{:S(2)}) collective-permute-start(f32[3,32,256]{2,1,0:T(8,128)S(1)} %add.3.refs_0_), channel_id=1, source_target_pairs={{0,1},{1,0},{2,3},{3,2},{4,5},{5,4},{6,7},{7,6},{8,9},{9,8},{10,11... | collective-permute-start | bytes 294920 | tf_op jit(solution)/shard_map/ppermute | solution.py:21
  61.4 6.1 %collective-permute-start.15 = (f32[3,32,256]{2,1,0:T(8,128)S(1)}, f32[3,32,256]{2,1,0:T(8,128)S(1)}, u32[]{:S(2)}, u32[]{:S(2)}) collective-permute-start(f32[3,32,256]{2,1,0:T(8,128)S(1)} %add.3.refs_0_), channel_id=1, source_target_pairs={{0,2},{1,3},{2,0},{3,1},{4,6},{5,7},{6,4},{7,5},{8,10},{9,11},{10,... | collective-permute-start | bytes 294920 | tf_op jit(solution)/shard_map/ppermute | solution.py:21
  63.0 6.2 %collective-permute-start.17 = (f32[3,32,256]{2,1,0:T(8,128)S(1)}, f32[3,32,256]{2,1,0:T(8,128)S(1)}, u32[]{:S(2)}, u32[]{:S(2)}) collective-permute-start(f32[3,32,256]{2,1,0:T(8,128)S(1)} %add.3.refs_0_), channel_id=1, source_target_pairs={{0,3},{1,2},{2,1},{3,0},{4,7},{5,6},{6,5},{7,4},{8,11},{9,10},{10,... | collective-permute-start | bytes 294920 | tf_op jit(solution)/shard_map/ppermute | solution.py:21
  64.4 5.7 %collective-permute-start.12 = (f32[3,32,256]{2,1,0:T(8,128)S(1)}, f32[3,32,256]{2,1,0:T(8,128)S(1)}, u32[]{:S(2)}, u32[]{:S(2)}) collective-permute-start(f32[3,32,256]{2,1,0:T(8,128)S(1)} %add.3.refs_0_), channel_id=1, source_target_pairs={{0,4},{4,0},{8,12},{12,8},{16,20},{20,16},{24,28},{28,24},{1,5},{5... | collective-permute-start | bytes 294920 | tf_op jit(solution)/shard_map/ppermute | solution.py:21
  66.6 3.6 %collective-permute-start.14 = (f32[3,32,256]{2,1,0:T(8,128)S(1)}, f32[3,32,256]{2,1,0:T(8,128)S(1)}, u32[]{:S(2)}, u32[]{:S(2)}) collective-permute-start(f32[3,32,256]{2,1,0:T(8,128)S(1)} %collective-permute-done.13.refs_2_), channel_id=1, source_target_pairs={{0,4},{4,0},{8,12},{12,8},{16,20},{20,16},{24,28},{28,24},{1,5},{5... | collective-permute-start | bytes 294920 | tf_op jit(solution)/shard_map/ppermute | solution.py:21
  (13 other events, 41.0 us)

commit v3 on v2

--- a/solution.py
+++ b/solution.py
@@ -33,6 +33,10 @@
     def one(a, b):
         return lax.dot_general(a, b, dims, preferred_element_type=F32)
 
+    if left_high.shape[0] <= W // 2 or left_high.shape == right_high.shape == (W, W):
+        (left_axis,), (right_axis,) = dims[0]
+        lefts = jnp.concatenate([left_high, left_low, left_high], axis=left_axis)
+        return one(lefts, jnp.concatenate([right_low, right_high, right_high], axis=right_axis))
     return one(left_high, right_low) + one(left_low, right_high) + one(left_high, right_high)
 
 
@@ -131,7 +135,7 @@
 
 def second_kernel(count, order_one, order_two, own, other, *refs):
     pieces, outs = refs[: 2 * count], refs[2 * count :]
-    inner_rows, inverse_out, coupling_inner, right_out, right_half, sums = outs
+    inner_rows, inverse_out, coupling_inner, sums = outs
     tree = Tree(order_one, order_two)
     half_width = pieces[0].shape[1]
     width = 2 * half_width
@@ -145,12 +149,9 @@
                 coupling_inner[target, :] = piece[1 + slot]
     inverse = newton(sums[...])
     inverse_out[...] = inverse
-    right = product(inverse, coupling_inner[...], NT)
-    right_out[...] = right
-    right_half[...] = right_out[pl.ds(pl.multiple_of(tree.half * (W // 2), W // 2), W // 2), :]
     start = pl.multiple_of(tree.half * half_width, half_width)
     left = jnp.concatenate([pieces[0][1], pieces[0][2]], axis=0)
-    change = product(left, right)
+    change = product(product(left, inverse), coupling_inner[...], NT)
     for slot, (row, column) in enumerate(((0, 0), (0, 1), (1, 1))):
         which, edge = tree.edge(4 + row)
         column_which, column_edge = tree.edge(4 + column)
@@ -159,10 +160,13 @@
         inner_rows[slot] = value - change[row * half_width : (row + 1) * half_width, column * W : (column + 1) * W]
 
 
-def outer_kernel(order_one, order_two, own, other, coupling, right, outer_all):
+def outer_kernel(order_one, order_two, own, other, coupling, inverse_one, coupling_inner, outer_all, right_out, right_half):
     tree = Tree(order_one, order_two)
     width = coupling.shape[1]
-    change = product(coupling[...].reshape(4 * width, W), right[...])
+    right = product(inverse_one[...], coupling_inner[...], NT)
+    right_out[...] = right
+    right_half[...] = right_out[pl.ds(pl.multiple_of(tree.half * (W // 2), W // 2), W // 2), :]
+    change = product(coupling[...].reshape(4 * width, W), right)
     for slot in range(4):
         base = interface_rows(tree, own, other, slot, 0, width)
         outer_all[slot] = base - change[slot * width : (slot + 1) * width]
@@ -209,15 +213,32 @@
             outer_half[rows, columns] = value - change[rows, columns]
 
 
-def near_kernel(count, order_one, order_two, own, other, coupling, inverse_one, right, *refs):
+def driven_by(tree, raws, data_half):
+    for mask, raw in enumerate(raws):
+        width = raw.shape[1]
+        at = (tree.member ^ mask) * width
+        for slot in range(2):
+            data_half[pl.ds(pl.multiple_of(slot * W + at, width), width), :] = raw[slot]
+    return parts_of(data_half[...].T)
+
+
+def share(tree, part, mine, theirs):
+    mine[...] = jnp.where(tree.half == 0, part[:2], part[2:])
+    theirs[...] = jnp.where(tree.half == 0, part[2:], part[:2])
+
+
+def near_kernel(count, order_one, order_two, own, other, coupling, inverse_one, right, outer_all, inverse_two, *refs):
     raws, outs = refs[:count], refs[count:]
-    base_out, outer_half, coupling_half, packed_zero, packed_one = outs
+    mine, theirs, scaled_out, driven, coupling_half, packed_zero, packed_one, outer_half, data_half, part = outs
     tree = Tree(order_one, order_two)
     width = own.shape[1]
     gathered(tree, [(raw.at[0:2], raw.at[2:4]) for raw in raws], coupling_half, packed_zero, packed_one)
     coupling_split = parts_of(coupling_half[...])
+    outer_rows(tree, tree.node, coupling_split, packed_zero, packed_one, right[...], outer_half)
+    outer_split = parts_of(outer_half[...])
+    scaled_out[...] = product(outer_all[...].reshape(4 * width, 2 * W), inverse_two[...])
     scaled = product(coupling[...].reshape(4 * width, W), inverse_one[...])
-    local = product(scaled, coupling_split, NT)
+    change = product(scaled, coupling_split, NT) + product(scaled_out[...], outer_split, NT)
     for slot in range(4):
         which, edge = tree.edge(slot)
         for column in range(2):
@@ -225,42 +246,31 @@
             value = block_of(tree, own, other, which, edge, 0, width, column_edge)
             value = jnp.where(which == column_which, value, 0.0)
             rows, columns = slice(slot * width, (slot + 1) * width), slice(column * W, (column + 1) * W)
-            base_out[slot, :, columns] = value - local[rows, columns]
-    outer_rows(tree, tree.node, coupling_split, packed_zero, packed_one, right[...], outer_half)
-
-
-def far_kernel(count, order_one, order_two, outer_near, coupling_near, right_mine, right_other, *refs):
-    raws, last, outs = refs[: 2 * count - 1], refs[2 * count - 1 : 2 * count + 2], refs[2 * count + 2 :]
-    datas = [raw.at[4:6] for raw in raws] + [last[2]]
+            part[slot, :, columns] = value - change[rows, columns]
+    share(tree, part, mine, theirs)
+    turned = driven_by(tree, [raw.at[4:6] for raw in raws], data_half)
+    driven[:, : 2 * W] = product(turned, outer_split)
+    driven[:, 2 * W :] = product(turned, coupling_split)
+
+
+def far_kernel(count, order_one, order_two, driven_near, right_mine, right_other, *refs):
+    raws, last, outs = refs[: count - 1], refs[count - 1 : count + 2], refs[count + 2 :]
     outer_half, driven, coupling_half, packed_zero, packed_one, right, data_half = outs
     tree = Tree(order_one, order_two)
-    pairs = [(raw.at[0:2], raw.at[2:4]) for raw in raws[count:]] + [last[:2]]
+    pairs = [(raw.at[0:2], raw.at[2:4]) for raw in raws] + [last[:2]]
     gathered(tree, pairs, coupling_half, packed_zero, packed_one)
     for side, held in enumerate((right_mine, right_other)):
         right[pl.ds(pl.multiple_of((tree.half ^ side) * (W // 2), W // 2), W // 2), :] = held[...]
     outer_rows(tree, tree.node ^ 1, parts_of(coupling_half[...]), packed_zero, packed_one, right[...], outer_half)
-    for place, data in enumerate(datas):
-        width = data.shape[1]
-        at = (tree.member ^ (place % count)) * width + (place // count) * 2 * W
-        for slot in range(2):
-            data_half[pl.ds(pl.multiple_of(slot * W + at, width), width), :] = data[slot]
-    near = parts_of(data_half[: 2 * W, :].T)
-    far = data_half[2 * W :, :].T
-    driven[:, : 2 * W] = product(near, outer_near[...]) + product(far, outer_half[...])
-    driven[:, 2 * W :] = product(near, coupling_near[...])
-
-
-def top_kernel(base, outer_all, inverse_two, outer_near, outer_far, mine, theirs):
-    half = lax.axis_index("leaf") % 2
-    slots, width, columns = base.shape
-    scaled = parts_of(product(outer_all[...].reshape(slots * width, columns), inverse_two[...]))
-    for far, outer in enumerate((outer_near, outer_far)):
-        part = -product(scaled, outer[...], NT).reshape(slots, width, columns)
-        if not far:
-            part = base[...] + part
-        target = slice(far * columns, (far + 1) * columns)
-        mine[:, :, target] = jnp.where(half == 0, part[:2], part[2:])
-        theirs[:, :, target] = jnp.where(half == 0, part[2:], part[:2])
+    turned = driven_by(tree, [raw.at[4:6] for raw in raws] + [last[2]], data_half)
+    driven[:, : 2 * W] = driven_near[:, : 2 * W] + product(turned, outer_half[...])
+    driven[:, 2 * W :] = driven_near[:, 2 * W :]
+
+
+def top_kernel(order_one, order_two, scaled, outer_far, mine, theirs):
+    tree = Tree(order_one, order_two)
+    part = -product(scaled[...], outer_far[...], NT)
+    share(tree, part.reshape(2 * mine.shape[0], mine.shape[1], mine.shape[2]), mine, theirs)
 
 
 def leaf_kernel(order_one, order_two, data_own, data_other, coupling_inner, inverse_one, inverse_two, driven, driven_other, leaf_data, inner):
@@ -285,14 +295,13 @@
         leaf_data[order_one[slot, tree.leaf]] = jnp.where(position < 4, from_data, from_inner)
 
 
-def join_kernel(mine, theirs, top_map):
+def join_kernel(mine_near, theirs_near, mine_far, theirs_far, top_map):
     half, node_bit = lax.axis_index("leaf") % 2, (lax.axis_index("leaf") // 2) % 2
-    columns = mine.shape[2] // 2
-    for far in range(2):
-        source = slice(far * columns, (far + 1) * columns)
-        for side, held in enumerate((mine, theirs)):
+    columns = mine_near.shape[2]
+    for far, pair in enumerate(((mine_near, theirs_near), (mine_far, theirs_far))):
+        for side, held in enumerate(pair):
             target = pl.multiple_of((2 * (node_bit ^ far) + (half ^ side)) * columns, columns)
-            top_map[:, :, pl.ds(target, columns)] = held[:, :, source]
+            top_map[:, :, pl.ds(target, columns)] = held[...]
 
 
 def call(kernel, scalar_count, outs, scratch, *args):
@@ -349,38 +358,43 @@
     pieces = with_sibling(across(piece))
     data_other = swapped(top_data, "leaf", 1)
     raws = spread(raw, [(2 * part, 2 * part + 2, part % len(bits)) for part in range(3)])
-    inner_rows, inverse_one, coupling_inner, right, right_half = call(
+    inner_rows, inverse_one, coupling_inner = call(
         lambda *refs: second_kernel(count, *refs), 2,
-        [(3, half_width, W), (W, W), (2 * W, W), (W, 2 * W), (W // 2, 2 * W)], [(W, W)],
+        [(3, half_width, W), (W, W), (2 * W, W)], [(W, W)],
         *orders, own, other, *pieces,
     )
     summed = inner_rows + swapped(inner_rows, "leaf", 2)
+    outer_all, right, right_half = call(
+        outer_kernel, 2, [(4, width, 2 * W), (W, 2 * W), (W // 2, 2 * W)], [],
+        *orders, own, other, coupling, inverse_one, coupling_inner,
+    )
     right_mine = swapped(right_half, "leaf", 2)
     right_other = swapped(right_mine, "leaf", 1)
-    (outer_all,) = call(outer_kernel, 2, [(4, width, 2 * W)], [], *orders, own, other, coupling, right)
     (inverse_two,) = call(
         lambda *refs: third_kernel(count, *refs), 0, [(2 * W, 2 * W)], [(2 * W, 2 * W)],
         *with_sibling(across(summed)),
     )
-    base, outer_near, coupling_near = call(
+    halves = [(2, width, 2 * W)] * 2
+    scratch = [(2 * W, W), (W, W), (W, W)]
+    mine_near, theirs_near, scaled, driven_near = call(
         lambda *refs: near_kernel(count, *refs), 2,
-        [(4, width, 2 * W), (2 * W, 2 * W), (2 * W, W)], [(W, W), (W, W)],
-        *orders, own, other, coupling, inverse_one, right, *raws[:count],
-    )
+        halves + [(4 * width, 2 * W), (K, 3 * W)], scratch + [(2 * W, 2 * W), (2 * W, K), (4, width, 2 * W)],
+        *orders, own, other, coupling, inverse_one, right, outer_all, inverse_two, *raws[:count],
+    )
+    received_near = swapped(theirs_near, "leaf", 1)
     outer_far, driven = call(
         lambda *refs: far_kernel(count, *refs), 2, [(2 * W, 2 * W), (K, 3 * W)],
-        [(2 * W, W), (W, W), (W, W), (W, 2 * W), (4 * W, K)],
-        *orders, outer_near, coupling_near, right_mine, right_other,
-        *raws[:-1], *raws[-1],
+        scratch + [(W, 2 * W), (2 * W, K)],
+        *orders, driven_near, right_mine, right_other, *raws[count:-1], *raws[-1],
     )
     driven_other = swapped(driven, "leaf", 1)
-    mine, theirs = call(top_kernel, 0, [(2, width, 4 * W)] * 2, [], base, outer_all, inverse_two, outer_near, outer_far)
-    received = swapped(theirs, "leaf", 1)
+    mine_far, theirs_far = call(top_kernel, 2, halves, [], *orders, scaled, outer_far)
+    received_far = swapped(theirs_far, "leaf", 1)
     (leaf_data,) = call(
         leaf_kernel, 2, [(4, width, K)], [(2 * width, K)],
         *orders, top_data, data_other, coupling_inner, inverse_one, inverse_two, driven, driven_other,
     )
-    (top_map,) = call(join_kernel, 0, [(2, width, 8 * W)], [], mine, received)
+    (top_map,) = call(join_kernel, 0, [(2, width, 8 * W)], [], mine_near, received_near, mine_far, received_far)
     return (top_map, leaf_data)
 
 

time: 83.8 us -> 84.1 us (level)
  starting transfers between devices: 24.2 us -> 22.9 us
  waiting for transfers between devices: 35.1 us -> 36.1 us
    ppermute x30 -> x31, starting transfers between devices: 24.2 us -> 22.9 us  [swapped(): return lax.ppermute(value, axis, pairs)]
    ppermute x30 -> x31, waiting for transfers between devices: 35.1 us -> 36.1 us  [swapped(): return lax.ppermute(value, axis, pairs)]
  transfers between devices with their start and end apart: 30 -> 31, of which waited for: 12 -> 10; matrix products, arithmetic and copies ran while one was open for 0% -> 0% of each run, Pallas kernels for 21% -> 19%
where the time goes in v3:
time: 84.1 us; the launch traced here: 83.9 us
  waiting for transfers between devices  36.1 us (43%)
  starting transfers between devices  22.9 us (27%)
  Pallas kernels  21.4 us (25%)
  local copies, waits for them, and re-layouts  2.71 us (3%)
    ppermute x31, waiting for transfers between devices, swapped(): return lax.ppermute(value, axis, pairs)  36.1 us
    ppermute x31, starting transfers between devices, swapped(): return lax.ppermute(value, axis, pairs)  22.9 us
    pallas_call x10, Pallas kernels, call(): pl.pallas_call(kernel, in_specs=[smem] * scalar_count + [vmem] * (len(arg...  21.4 us
    unnamed x14, local copies, waits for them, and re-layouts  2.68 us
  transfers between devices with their start and end apart: 31, of which 10 were waited for; matrix products, arithmetic and copies ran while one was open for 0% of the time, Pallas kernels for 19%

profile of v3, /device:TPU:0, one launch (start us, length us, event | category | flops | bytes accessed | tf_op | source)
XLA Modules:
  0.0 83.9 jit_solution(14886929961156219539)
XLA Ops:
  5.5 2.6 %collective-permute-start.17 = (f32[6,64,256]{2,1,0:T(8,128)S(1)}, f32[6,64,256]{2,1,0:T(8,128)S(1)}, u32[]{:S(2)}, u32[]{:S(2)}) collective-permute-start(f32[6,64,256]{2,1,0:T(8,128)S(1)} %get-tuple-element.32.refs_9_), channel_id=1, source_target_pairs={{0,2},{1,3},{2,0},{3,1},{4,6},{5,7},{6,4},{7,5},{8,10},{9,11},{10,... | collective-permute-start | bytes 1179656 | tf_op jit(solution)/shard_map/ppermute | solution.py:21
  8.0 1.6 %collective-permute-start.22 = (f32[6,64,256]{2,1,0:T(8,128)S(1)}, f32[6,64,256]{2,1,0:T(8,128)S(1)}, u32[]{:S(2)}, u32[]{:S(2)}) collective-permute-start(f32[6,64,256]{2,1,0:T(8,128)S(1)} %get-tuple-element.32.refs_9_), channel_id=1, source_target_pairs={{0,8},{4,12},{8,0},{12,4},{16,24},{20,28},{24,16},{28,20},{1,9},{5... | collective-permute-start | bytes 1179656 | tf_op jit(solution)/shard_map/ppermute | solution.py:21
  9.6 1.5 %collective-permute-start.16 = (f32[6,64,256]{2,1,0:T(8,128)S(1)}, f32[6,64,256]{2,1,0:T(8,128)S(1)}, u32[]{:S(2)}, u32[]{:S(2)}) collective-permute-start(f32[6,64,256]{2,1,0:T(8,128)S(1)} %get-tuple-element.32.refs_9_), channel_id=1, source_target_pairs={{0,1},{1,0},{2,3},{3,2},{4,5},{5,4},{6,7},{7,6},{8,9},{9,8},{10,11... | collective-permute-start | bytes 1179656 | tf_op jit(solution)/shard_map/ppermute | solution.py:21
  12.2 10.5 %collective-permute-done.2.refs_6_ = f32[3,32,256]{2,1,0:T(8,128)S(1)} collective-permute-done((f32[3,32,256]{2,1,0:T(8,128)S(1)}, f32[3,32,256]{2,1,0:T(8,128)S(1)}, u32[]{:S(2)}, u32[]{:S(2)}) %collective-permute-start.2) | collective-permute-done | bytes 98336 | tf_op jit(solution)/shard_map/ppermute | solution.py:21
  22.7 1.4 %collective-permute-start.6 = (f32[3,32,256]{2,1,0:T(8,128)S(1)}, f32[3,32,256]{2,1,0:T(8,128)S(1)}, u32[]{:S(2)}, u32[]{:S(2)}) collective-permute-start(f32[3,32,256]{2,1,0:T(8,128)S(1)} %get-tuple-element.26.refs_4_), channel_id=1, source_target_pairs={{0,3},{1,2},{2,1},{3,0},{4,7},{5,6},{6,5},{7,4},{8,11},{9,10},{10,... | collective-permute-start | bytes 294920 | tf_op jit(solution)/shard_map/ppermute | solution.py:21
  24.1 4.1 %collective-permute-done.6.refs_10_ = f32[3,32,256]{2,1,0:T(8,128)S(1)} collective-permute-done((f32[3,32,256]{2,1,0:T(8,128)S(1)}, f32[3,32,256]{2,1,0:T(8,128)S(1)}, u32[]{:S(2)}, u32[]{:S(2)}) %collective-permute-start.6) | collective-permute-done | bytes 98336 | tf_op jit(solution)/shard_map/ppermute | solution.py:21
  29.7 1.5 %collective-permute-start.18 = (f32[6,64,256]{2,1,0:T(8,128)S(1)}, f32[6,64,256]{2,1,0:T(8,128)S(1)}, u32[]{:S(2)}, u32[]{:S(2)}) collective-permute-start(f32[6,64,256]{2,1,0:T(8,128)S(1)} %collective-permute-done.17.refs_11_), channel_id=1, source_target_pairs={{0,1},{1,0},{2,3},{3,2},{4,5},{5,4},{6,7},{7,6},{8,9},{9,8},{10,11... | collective-permute-start | bytes 1179656 | tf_op jit(solution)/shard_map/ppermute | solution.py:21
  32.1 2.6 %shard_map.61 = (f32[3,32,256]{2,1,0:T(8,128)S(1)}, f32[256,256]{1,0:T(8,128)S(1)}, f32[512,256]{1,0:T(8,128)S(1)}) custom-call(s32[4,8]{1,0:T(4,128)S(1)} %bitcast.3, s32[4,6]{1,0:T(4,128)S(1)} %copy-done.5, f32[4,64,1024]{2,1,0:T(8,128)S(1)} %copy-done.1, f32[4,64,1024]{2,1,0:T(8,128)S(1)} %collective-permute-done.refs_2_.refs_3_.other, ...), custom_call_target="tpu_custom_call" | custom-call | tf_op jit(solution)/shard_map/pallas_call | solution.py:310
  34.7 1.6 %collective-permute-start.8 = (f32[3,32,256]{2,1,0:T(8,128)S(1)}, f32[3,32,256]{2,1,0:T(8,128)S(1)}, u32[]{:S(2)}, u32[]{:S(2)}) collective-permute-start(f32[3,32,256]{2,1,0:T(8,128)S(1)} %get-tuple-element.31), channel_id=1, source_target_pairs={{0,8},{4,12},{8,0},{12,4},{16,24},{20,28},{24,16},{28,20},{1,9},{5... | collective-permute-start | bytes 294920 | tf_op jit(solution)/shard_map/ppermute | solution.py:21
  36.4 1.4 %shard_map.62 = (f32[4,64,512]{2,1,0:T(8,128)S(1)}, f32[256,512]{1,0:T(8,128)S(1)}, f32[128,512]{1,0:T(8,128)S(1)}) custom-call(s32[4,8]{1,0:T(4,128)S(1)} %bitcast.4, s32[4,6]{1,0:T(4,128)S(1)} %copy-done.5, f32[4,64,1024]{2,1,0:T(8,128)S(1)} %copy-done.1, f32[4,64,1024]{2,1,0:T(8,128)S(1)} %collective-permute-done.refs_2_.refs_3_.other, ...), custom_call_target="tpu_custom_call" | custom-call | tf_op jit(solution)/shard_map/pallas_call | solution.py:310
  38.3 7.4 %collective-permute-done.8 = f32[3,32,256]{2,1,0:T(8,128)S(1)} collective-permute-done((f32[3,32,256]{2,1,0:T(8,128)S(1)}, f32[3,32,256]{2,1,0:T(8,128)S(1)}, u32[]{:S(2)}, u32[]{:S(2)}) %collective-permute-start.8) | collective-permute-done | bytes 98336 | tf_op jit(solution)/shard_map/ppermute | solution.py:21
  46.4 4.1 %collective-permute-done.10.refs_2_ = f32[3,32,256]{2,1,0:T(8,128)S(1)} collective-permute-done((f32[3,32,256]{2,1,0:T(8,128)S(1)}, f32[3,32,256]{2,1,0:T(8,128)S(1)}, u32[]{:S(2)}, u32[]{:S(2)}) %collective-permute-start.10) | collective-permute-done | bytes 98336 | tf_op jit(solution)/shard_map/ppermute | solution.py:21
  50.5 1.5 %collective-permute-start.12 = (f32[3,32,256]{2,1,0:T(8,128)S(1)}, f32[3,32,256]{2,1,0:T(8,128)S(1)}, u32[]{:S(2)}, u32[]{:S(2)}) collective-permute-start(f32[3,32,256]{2,1,0:T(8,128)S(1)} %add.3.refs_0_), channel_id=1, source_target_pairs={{0,2},{1,3},{2,0},{3,1},{4,6},{5,7},{6,4},{7,5},{8,10},{9,11},{10,... | collective-permute-start | bytes 294920 | tf_op jit(solution)/shard_map/ppermute | solution.py:21
  52.0 3.1 %collective-permute-done.12.refs_4_ = f32[3,32,256]{2,1,0:T(8,128)S(1)} collective-permute-done((f32[3,32,256]{2,1,0:T(8,128)S(1)}, f32[3,32,256]{2,1,0:T(8,128)S(1)}, u32[]{:S(2)}, u32[]{:S(2)}) %collective-permute-start.12) | collective-permute-done | bytes 98336 | tf_op jit(solution)/shard_map/ppermute | solution.py:21
  55.1 1.5 %collective-permute-start.14 = (f32[3,32,256]{2,1,0:T(8,128)S(1)}, f32[3,32,256]{2,1,0:T(8,128)S(1)}, u32[]{:S(2)}, u32[]{:S(2)}) collective-permute-start(f32[3,32,256]{2,1,0:T(8,128)S(1)} %add.3.refs_0_), channel_id=1, source_target_pairs={{0,3},{1,2},{2,1},{3,0},{4,7},{5,6},{6,5},{7,4},{8,11},{9,10},{10,... | collective-permute-start | bytes 294920 | tf_op jit(solution)/shard_map/ppermute | solution.py:21
  57.2 3.7 %collective-permute-done.14.refs_6_ = f32[3,32,256]{2,1,0:T(8,128)S(1)} collective-permute-done((f32[3,32,256]{2,1,0:T(8,128)S(1)}, f32[3,32,256]{2,1,0:T(8,128)S(1)}, u32[]{:S(2)}, u32[]{:S(2)}) %collective-permute-start.14) | collective-permute-done | bytes 98336 | tf_op jit(solution)/shard_map/ppermute | solution.py:21
  61.1 1.5 %collective-permute-start.26 = (f32[2,64,256]{2,1,0:T(8,128)S(1)}, f32[2,64,256]{2,1,0:T(8,128)S(1)}, u32[]{:S(2)}, u32[]{:S(2)}) collective-permute-start(f32[2,64,256]{2,1,0:T(8,128)S(1)} %slice.13), channel_id=1, source_target_pairs={{0,2},{1,3},{2,0},{3,1},{4,6},{5,7},{6,4},{7,5},{8,10},{9,11},{10,... | collective-permute-start | bytes 393224 | tf_op jit(solution)/shard_map/ppermute | solution.py:21
  62.7 1.9 %collective-permute-start.27 = (f32[2,64,256]{2,1,0:T(8,128)S(1)}, f32[2,64,256]{2,1,0:T(8,128)S(1)}, u32[]{:S(2)}, u32[]{:S(2)}) collective-permute-start(f32[2,64,256]{2,1,0:T(8,128)S(1)} %slice.14), channel_id=1, source_target_pairs={{0,8},{4,12},{8,0},{12,4},{16,24},{20,28},{24,16},{28,20},{1,9},{5... | collective-permute-start | bytes 393224 | tf_op jit(solution)/shard_map/ppermute | solution.py:21
  64.6 1.3 %collective-permute-done.15.refs_7_ = f32[3,32,256]{2,1,0:T(8,128)S(1)} collective-permute-done((f32[3,32,256]{2,1,0:T(8,128)S(1)}, f32[3,32,256]{2,1,0:T(8,128)S(1)}, u32[]{:S(2)}, u32[]{:S(2)}) %collective-permute-start.15) | collective-permute-done | bytes 98336 | tf_op jit(solution)/shard_map/ppermute | solution.py:21
  65.9 5.7 %shard_map.63.refs_8_.inverse_two = f32[512,512]{1,0:T(8,128)S(1)} custom-call(f32[3,32,256]{2,1,0:T(8,128)S(1)} %add.3.refs_0_, f32[3,32,256]{2,1,0:T(8,128)S(1)} %collective-permute-done.9.refs_1_, f32[3,32,256]{2,1,0:T(8,128)S(1)} %collective-permute-done.10.refs_2_, f32[3,32,256]{2,1,0:T(8,128)S(1)} %collective-permute-done.11.refs_3_, ...), custom_call_target="tpu_custom_call" | custom-call | tf_op jit(solution)/shard_map/pallas_call | solution.py:310
  71.6 3.2 %shard_map.64 = (f32[2,64,512]{2,1,0:T(8,128)S(1)}, f32[2,64,512]{2,1,0:T(8,128)S(1)}, f32[256,512]{1,0:T(8,128)S(1)}, f32[256,768]{1,0:T(8,128)S(1)}) custom-call(s32[4,8]{1,0:T(4,128)S(1)} %bitcast.5, s32[4,6]{1,0:T(4,128)S(1)} %copy-done.5, f32[4,64,1024]{2,1,0:T(8,128)S(1)} %copy-done.1, f32[4,64,1024]{2,1,0:T(8,128)S(1)} %collective-permute-done.refs_2_.refs_3_.other, ...), custom_call_target="tpu_custom_call" | custom-call | tf_op jit(solution)/shard_map/pallas_call | solution.py:310
  74.8 1.8 %shard_map.65 = (f32[512,512]{1,0:T(8,128)S(1)}, f32[256,768]{1,0:T(8,128)S(1)}) custom-call(s32[4,8]{1,0:T(4,128)S(1)} %bitcast.6, s32[4,6]{1,0:T(4,128)S(1)} %copy-done.5, f32[256,768]{1,0:T(8,128)S(1)} %get-tuple-element.36.refs_2_, f32[128,512]{1,0:T(8,128)S(1)} %collective-permute-done.20.refs_3_, f32[128,512]{1,0:T(8,128)S(1)} %collective-permute-done.21.refs_4_, ...), custom_call_target="tpu_custom_call" | custom-call | tf_op jit(solution)/shard_map/pallas_call | solution.py:310
  77.2 1.2 %shard_map.66 = (f32[2,64,512]{2,1,0:T(8,128)S(1)}, f32[2,64,512]{2,1,0:T(8,128)S(1)}) custom-call(s32[4,8]{1,0:T(4,128)S(1)} %bitcast.7, s32[4,6]{1,0:T(4,128)S(1)} %copy-done.5, f32[256,512]{1,0:T(8,128)S(1)} %get-tuple-element.35.scaled, f32[512,512]{1,0:T(8,128)S(1)} %get-tuple-element.38.outer_far), custom_call_target="tpu_custom_call" | custom-call | tf_op jit(solution)/shard_map/pallas_call | solution.py:310
  81.2 2.7 %shard_map.68 = f32[4,64,256]{2,1,0:T(8,128)} custom-call(s32[4,8]{1,0:T(4,128)S(1)} %bitcast.8, s32[4,6]{1,0:T(4,128)S(1)} %copy-done.6, f32[2,64,256]{2,1,0:T(8,128)S(1)} %copy-done.2, f32[2,64,256]{2,1,0:T(8,128)S(1)} %collective-permute-done.29.data_other, f32[512,256]{1,0:T(8,128)S(1)} %get-tuple-element.28.coupling_inner, ...), custom_call_target="tpu_custom_call" | custom-call | tf_op jit(solution)/shard_map/pallas_call | solution.py:310
  (66 shorter events, 13.5 us)
Async XLA Ops:
  0.6 4.0 %collective-permute-start = (f32[4,64,1024]{2,1,0:T(8,128)}, f32[4,64,1024]{2,1,0:T(8,128)S(1)}, u32[]{:S(2)}, u32[]{:S(2)}) collective-permute-start(f32[4,64,1024]{2,1,0:T(8,128)} %refs_2_.5), channel_id=1, source_target_pairs={{0,4},{4,0},{8,12},{12,8},{16,20},{20,16},{24,28},{28,24},{1,5},{5... | collective-permute-start | bytes 3145736 | tf_op jit(solution)/shard_map/ppermute | solution.py:21
  5.5 24.2 %collective-permute-start.17 = (f32[6,64,256]{2,1,0:T(8,128)S(1)}, f32[6,64,256]{2,1,0:T(8,128)S(1)}, u32[]{:S(2)}, u32[]{:S(2)}) collective-permute-start(f32[6,64,256]{2,1,0:T(8,128)S(1)} %get-tuple-element.32.refs_9_), channel_id=1, source_target_pairs={{0,2},{1,3},{2,0},{3,1},{4,6},{5,7},{6,4},{7,5},{8,10},{9,11},{10,... | collective-permute-start | bytes 1179656 | tf_op jit(solution)/shard_map/ppermute | solution.py:21
  8.0 23.1 %collective-permute-start.22 = (f32[6,64,256]{2,1,0:T(8,128)S(1)}, f32[6,64,256]{2,1,0:T(8,128)S(1)}, u32[]{:S(2)}, u32[]{:S(2)}) collective-permute-start(f32[6,64,256]{2,1,0:T(8,128)S(1)} %get-tuple-element.32.refs_9_), channel_id=1, source_target_pairs={{0,8},{4,12},{8,0},{12,4},{16,24},{20,28},{24,16},{28,20},{1,9},{5... | collective-permute-start | bytes 1179656 | tf_op jit(solution)/shard_map/ppermute | solution.py:21
  9.6 22.0 %collective-permute-start.16 = (f32[6,64,256]{2,1,0:T(8,128)S(1)}, f32[6,64,256]{2,1,0:T(8,128)S(1)}, u32[]{:S(2)}, u32[]{:S(2)}) collective-permute-start(f32[6,64,256]{2,1,0:T(8,128)S(1)} %get-tuple-element.32.refs_9_), channel_id=1, source_target_pairs={{0,1},{1,0},{2,3},{3,2},{4,5},{5,4},{6,7},{7,6},{8,9},{9,8},{10,11... | collective-permute-start | bytes 1179656 | tf_op jit(solution)/shard_map/ppermute | solution.py:21
  11.1 11.6 %collective-permute-start.2 = (f32[3,32,256]{2,1,0:T(8,128)S(1)}, f32[3,32,256]{2,1,0:T(8,128)S(1)}, u32[]{:S(2)}, u32[]{:S(2)}) collective-permute-start(f32[3,32,256]{2,1,0:T(8,128)S(1)} %get-tuple-element.26.refs_4_), channel_id=1, source_target_pairs={{0,1},{1,0},{2,3},{3,2},{4,5},{5,4},{6,7},{7,6},{8,9},{9,8},{10,11... | collective-permute-start | bytes 294920 | tf_op jit(solution)/shard_map/ppermute | solution.py:21
  11.6 12.5 %collective-permute-start.4 = (f32[3,32,256]{2,1,0:T(8,128)S(1)}, f32[3,32,256]{2,1,0:T(8,128)S(1)}, u32[]{:S(2)}, u32[]{:S(2)}) collective-permute-start(f32[3,32,256]{2,1,0:T(8,128)S(1)} %get-tuple-element.26.refs_4_), channel_id=1, source_target_pairs={{0,2},{1,3},{2,0},{3,1},{4,6},{5,7},{6,4},{7,5},{8,10},{9,11},{10,... | collective-permute-start | bytes 294920 | tf_op jit(solution)/shard_map/ppermute | solution.py:21
  22.7 5.5 %collective-permute-start.6 = (f32[3,32,256]{2,1,0:T(8,128)S(1)}, f32[3,32,256]{2,1,0:T(8,128)S(1)}, u32[]{:S(2)}, u32[]{:S(2)}) collective-permute-start(f32[3,32,256]{2,1,0:T(8,128)S(1)} %get-tuple-element.26.refs_4_), channel_id=1, source_target_pairs={{0,3},{1,2},{2,1},{3,0},{4,7},{5,6},{6,5},{7,4},{8,11},{9,10},{10,... | collective-permute-start | bytes 294920 | tf_op jit(solution)/shard_map/ppermute | solution.py:21
  24.1 4.1 %collective-permute-start.1 = (f32[3,32,256]{2,1,0:T(8,128)S(1)}, f32[3,32,256]{2,1,0:T(8,128)S(1)}, u32[]{:S(2)}, u32[]{:S(2)}) collective-permute-start(f32[3,32,256]{2,1,0:T(8,128)S(1)} %get-tuple-element.26.refs_4_), channel_id=1, source_target_pairs={{0,4},{4,0},{8,12},{12,8},{16,20},{20,16},{24,28},{28,24},{1,5},{5... | collective-permute-start | bytes 294920 | tf_op jit(solution)/shard_map/ppermute | solution.py:21
  29.7 26.9 %collective-permute-start.18 = (f32[6,64,256]{2,1,0:T(8,128)S(1)}, f32[6,64,256]{2,1,0:T(8,128)S(1)}, u32[]{:S(2)}, u32[]{:S(2)}) collective-permute-start(f32[6,64,256]{2,1,0:T(8,128)S(1)} %collective-permute-done.17.refs_11_), channel_id=1, source_target_pairs={{0,1},{1,0},{2,3},{3,2},{4,5},{5,4},{6,7},{7,6},{8,9},{9,8},{10,11... | collective-permute-start | bytes 1179656 | tf_op jit(solution)/shard_map/ppermute | solution.py:21
  31.2 25.4 %collective-permute-start.24 = (f32[6,64,256]{2,1,0:T(8,128)S(1)}, f32[6,64,256]{2,1,0:T(8,128)S(1)}, u32[]{:S(2)}, u32[]{:S(2)}) collective-permute-start(f32[6,64,256]{2,1,0:T(8,128)S(1)} %collective-permute-done.22.refs_5_), channel_id=1, source_target_pairs={{0,2},{1,3},{2,0},{3,1},{4,6},{5,7},{6,4},{7,5},{8,10},{9,11},{10,... | collective-permute-start | bytes 1179656 | tf_op jit(solution)/shard_map/ppermute | solution.py:21
  31.7 25.4 %collective-permute-start.23 = (f32[6,64,256]{2,1,0:T(8,128)S(1)}, f32[6,64,256]{2,1,0:T(8,128)S(1)}, u32[]{:S(2)}, u32[]{:S(2)}) collective-permute-start(f32[6,64,256]{2,1,0:T(8,128)S(1)} %collective-permute-done.16.refs_10_), channel_id=1, source_target_pairs={{0,8},{4,12},{8,0},{12,4},{16,24},{20,28},{24,16},{28,20},{1,9},{5... | collective-permute-start | bytes 1179656 | tf_op jit(solution)/shard_map/ppermute | solution.py:21
  34.7 11.0 %collective-permute-start.8 = (f32[3,32,256]{2,1,0:T(8,128)S(1)}, f32[3,32,256]{2,1,0:T(8,128)S(1)}, u32[]{:S(2)}, u32[]{:S(2)}) collective-permute-start(f32[3,32,256]{2,1,0:T(8,128)S(1)} %get-tuple-element.31), channel_id=1, source_target_pairs={{0,8},{4,12},{8,0},{12,4},{16,24},{20,28},{24,16},{28,20},{1,9},{5... | collective-permute-start | bytes 294920 | tf_op jit(solution)/shard_map/ppermute | solution.py:21
  37.8 14.2 %collective-permute-start.20 = (f32[128,512]{1,0:T(8,128)S(1)}, f32[128,512]{1,0:T(8,128)S(1)}, u32[]{:S(2)}, u32[]{:S(2)}) collective-permute-start(f32[128,512]{1,0:T(8,128)S(1)} %get-tuple-element.37), channel_id=1, source_target_pairs={{0,8},{4,12},{8,0},{12,4},{16,24},{20,28},{24,16},{28,20},{1,9},{5... | collective-permute-start | bytes 786440 | tf_op jit(solution)/shard_map/ppermute | solution.py:21
  45.8 4.7 %collective-permute-start.10 = (f32[3,32,256]{2,1,0:T(8,128)S(1)}, f32[3,32,256]{2,1,0:T(8,128)S(1)}, u32[]{:S(2)}, u32[]{:S(2)}) collective-permute-start(f32[3,32,256]{2,1,0:T(8,128)S(1)} %add.3.refs_0_), channel_id=1, source_target_pairs={{0,1},{1,0},{2,3},{3,2},{4,5},{5,4},{6,7},{7,6},{8,9},{9,8},{10,11... | collective-permute-start | bytes 294920 | tf_op jit(solution)/shard_map/ppermute | solution.py:21
  50.5 4.6 %collective-permute-start.12 = (f32[3,32,256]{2,1,0:T(8,128)S(1)}, f32[3,32,256]{2,1,0:T(8,128)S(1)}, u32[]{:S(2)}, u32[]{:S(2)}) collective-permute-start(f32[3,32,256]{2,1,0:T(8,128)S(1)} %add.3.refs_0_), channel_id=1, source_target_pairs={{0,2},{1,3},{2,0},{3,1},{4,6},{5,7},{6,4},{7,5},{8,10},{9,11},{10,... | collective-permute-start | bytes 294920 | tf_op jit(solution)/shard_map/ppermute | solution.py:21
  52.0 22.8 %collective-permute-start.21 = (f32[128,512]{1,0:T(8,128)S(1)}, f32[128,512]{1,0:T(8,128)S(1)}, u32[]{:S(2)}, u32[]{:S(2)}) collective-permute-start(f32[128,512]{1,0:T(8,128)S(1)} %collective-permute-done.20.refs_3_), channel_id=1, source_target_pairs={{0,4},{4,0},{8,12},{12,8},{16,20},{20,16},{24,28},{28,24},{1,5},{5... | collective-permute-start | bytes 786440 | tf_op jit(solution)/shard_map/ppermute | solution.py:21
  55.1 5.8 %collective-permute-start.14 = (f32[3,32,256]{2,1,0:T(8,128)S(1)}, f32[3,32,256]{2,1,0:T(8,128)S(1)}, u32[]{:S(2)}, u32[]{:S(2)}) collective-permute-start(f32[3,32,256]{2,1,0:T(8,128)S(1)} %add.3.refs_0_), channel_id=1, source_target_pairs={{0,3},{1,2},{2,1},{3,0},{4,7},{5,6},{6,5},{7,4},{8,11},{9,10},{10,... | collective-permute-start | bytes 294920 | tf_op jit(solution)/shard_map/ppermute | solution.py:21
  56.6 4.5 %collective-permute-start.9 = (f32[3,32,256]{2,1,0:T(8,128)S(1)}, f32[3,32,256]{2,1,0:T(8,128)S(1)}, u32[]{:S(2)}, u32[]{:S(2)}) collective-permute-start(f32[3,32,256]{2,1,0:T(8,128)S(1)} %add.3.refs_0_), channel_id=1, source_target_pairs={{0,4},{4,0},{8,12},{12,8},{16,20},{20,16},{24,28},{28,24},{1,5},{5... | collective-permute-start | bytes 294920 | tf_op jit(solution)/shard_map/ppermute | solution.py:21
  56.6 6.1 %collective-permute-start.11 = (f32[3,32,256]{2,1,0:T(8,128)S(1)}, f32[3,32,256]{2,1,0:T(8,128)S(1)}, u32[]{:S(2)}, u32[]{:S(2)}) collective-permute-start(f32[3,32,256]{2,1,0:T(8,128)S(1)} %collective-permute-done.10.refs_2_), channel_id=1, source_target_pairs={{0,4},{4,0},{8,12},{12,8},{16,20},{20,16},{24,28},{28,24},{1,5},{5... | collective-permute-start | bytes 294920 | tf_op jit(solution)/shard_map/ppermute | solution.py:21
  57.1 7.5 %collective-permute-start.13 = (f32[3,32,256]{2,1,0:T(8,128)S(1)}, f32[3,32,256]{2,1,0:T(8,128)S(1)}, u32[]{:S(2)}, u32[]{:S(2)}) collective-permute-start(f32[3,32,256]{2,1,0:T(8,128)S(1)} %collective-permute-done.12.refs_4_), channel_id=1, source_target_pairs={{0,4},{4,0},{8,12},{12,8},{16,20},{20,16},{24,28},{28,24},{1,5},{5... | collective-permute-start | bytes 294920 | tf_op jit(solution)/shard_map/ppermute | solution.py:21
  60.9 13.9 %collective-permute-start.25 = (f32[2,64,256]{2,1,0:T(8,128)S(1)}, f32[2,64,256]{2,1,0:T(8,128)S(1)}, u32[]{:S(2)}, u32[]{:S(2)}) collective-permute-start(f32[2,64,256]{2,1,0:T(8,128)S(1)} %slice.12), channel_id=1, source_target_pairs={{0,1},{1,0},{2,3},{3,2},{4,5},{5,4},{6,7},{7,6},{8,9},{9,8},{10,11... | collective-permute-start | bytes 393224 | tf_op jit(solution)/shard_map/ppermute | solution.py:21
  61.1 13.7 %collective-permute-start.26 = (f32[2,64,256]{2,1,0:T(8,128)S(1)}, f32[2,64,256]{2,1,0:T(8,128)S(1)}, u32[]{:S(2)}, u32[]{:S(2)}) collective-permute-start(f32[2,64,256]{2,1,0:T(8,128)S(1)} %slice.13), channel_id=1, source_target_pairs={{0,2},{1,3},{2,0},{3,1},{4,6},{5,7},{6,4},{7,5},{8,10},{9,11},{10,... | collective-permute-start | bytes 393224 | tf_op jit(solution)/shard_map/ppermute | solution.py:21
  62.7 12.1 %collective-permute-start.27 = (f32[2,64,256]{2,1,0:T(8,128)S(1)}, f32[2,64,256]{2,1,0:T(8,128)S(1)}, u32[]{:S(2)}, u32[]{:S(2)}) collective-permute-start(f32[2,64,256]{2,1,0:T(8,128)S(1)} %slice.14), channel_id=1, source_target_pairs={{0,8},{4,12},{8,0},{12,4},{16,24},{20,28},{24,16},{28,20},{1,9},{5... | collective-permute-start | bytes 393224 | tf_op jit(solution)/shard_map/ppermute | solution.py:21
  76.7 4.5 %collective-permute-start.30 = (f32[256,768]{1,0:T(8,128)S(1)}, f32[256,768]{1,0:T(8,128)S(1)}, u32[]{:S(2)}, u32[]{:S(2)}) collective-permute-start(f32[256,768]{1,0:T(8,128)S(1)} %get-tuple-element.41.driven), channel_id=1, source_target_pairs={{0,4},{4,0},{8,12},{12,8},{16,20},{20,16},{24,28},{28,24},{1,5},{5... | collective-permute-start | bytes 2359304 | tf_op jit(solution)/shard_map/ppermute | solution.py:21
  (14 other events, 48.9 us)
